TPU v7x, 256 devices: a whole 4x4x8 slice. The times are simulated.
256 devices in a mesh: rows: 64 (over z, x, core), cols: 4 (over y).
Axes of the slice: x: 4, y: 4, z: 8, core: 2. Of those that a mesh axis runs over, the one named last changes fastest.
Arguments:
- embeddings: bfloat16 [65536, 512], P('rows'), may hold values from -90 to 90
- neighbours: int32 [256, 12], P('rows'), may hold values from -1 to 255, as said below
- queries: float32 [65536, 512], P('rows', 'cols'), may hold values from -22 to 22
Outputs:
- diffused: float32 [65536, 512], P('rows', 'cols')
Inputs may be any that keep to these rules, and one draw needn't show every extreme that they name: `neighbours`: row b lists in rising order the distinct blocks linked to block b, then -1 in the remaining slots. Every block is linked to itself, links are symmetric, and a linked block lies on the same index of rows as b or on an adjacent one, block c lying on index c // 4. Some block has 12 links.
All inputs are finite; a program needn't handle non-finite values.
Results may differ from a plain program's by a relative error of at most 0.00039.
Values may be sent and summed in bfloat16 or wider, within the bound.
No kernel may reach another device: no remote copies, remote signals or barrier semaphores. Data moves between devices by JAX's collectives and lax.ppermute only.
A program may use at most 128 MiB of HBM per device.

v0:
```python
import jax
import jax.numpy as jnp
from jax import lax
from jax.sharding import PartitionSpec as P

ITERS = 3


diffusion = 0.9
epsilon = 1e-06
highest = lax.Precision.HIGHEST
contract_rows = (((1,), (1,)), ((), ()))


def extended(array, sides, width):
    for axis, dim in sides:
        peers, length = (lax.axis_size(axis), array.shape[dim])
        up = [(i, (i + 1) % peers) for i in range(peers - 1)]
        down = [(j, i) for i, j in up]
        last = lax.slice_in_dim(array, length - width, length, axis=dim)
        leading = lax.slice_in_dim(array, 0, width, axis=dim)
        before = lax.ppermute(last, axis, up)
        after = lax.ppermute(leading, axis, down)
        array = jnp.concatenate([before, array, after], axis=dim)
    return array


def column_sums(left_side, right_side):
    return jnp.sum(left_side * right_side, axis=0)


def squares(residual):
    return lax.psum(column_sums(residual, residual), "rows")


def shards(embeddings, neighbours, queries):
    own_blocks = neighbours.shape[0]
    own_rows = embeddings.shape[0]
    block_rows = own_rows // own_blocks
    features = embeddings.shape[1]
    values = embeddings.astype(jnp.float32)
    normed = (values * lax.rsqrt(jnp.sum(values * values, axis=1, keepdims=True) + epsilon)).astype(
        jnp.bfloat16
    )
    stacked = normed.reshape(own_blocks, block_rows, features)
    beside_all = extended(stacked, (("rows", 0),), own_blocks)
    similar = lax.dot_general(
        normed,
        beside_all.reshape(3 * own_rows, features),
        contract_rows,
        preferred_element_type=jnp.float32,
    )
    lowest = (lax.axis_index("rows") - 1) * own_blocks
    candidates = lowest + jnp.arange(3 * own_blocks, dtype=jnp.int32)
    linked = jnp.any(neighbours[:, :, None] == candidates[None, None, :], axis=1).astype(
        jnp.float32
    )
    cubed = jnp.maximum(similar, 0.0) ** 3
    affinity = (
        cubed.reshape(own_blocks, block_rows, 3 * own_blocks, block_rows) * linked[:, None, :, None]
    ).reshape(own_rows, 3 * own_rows)
    inv_root = lax.rsqrt(jnp.sum(affinity, axis=1))
    far_roots = extended(inv_root.reshape(own_blocks, block_rows), (("rows", 0),), own_blocks)
    banded = affinity * inv_root[:, None] * far_roots.reshape(1, 3 * own_rows)
    solution = jnp.zeros_like(queries)
    residual = queries
    direction = queries
    residual_sq = squares(residual)
    for iteration in range(ITERS):
        columns = direction.shape[1]
        outgoing = direction
        nearby = extended(
            outgoing.reshape(own_blocks, block_rows, columns), (("rows", 0),), own_blocks
        )
        mixed = jnp.dot(
            banded,
            nearby.reshape(3 * own_rows, columns),
            precision=highest,
            preferred_element_type=jnp.float32,
        )
        image = direction - diffusion * mixed
        curvature = lax.psum(column_sums(direction, image), "rows")
        step_size = residual_sq / curvature
        solution = solution + step_size * direction
        residual = residual - step_size * image
        if iteration + 1 < ITERS:
            updated = squares(residual)
            direction = residual + updated / residual_sq * direction
            residual_sq = updated
    return solution


def solution(mesh):
    placed = (P("rows", None), P("rows", None), P("rows", "cols"))
    return jax.shard_map(
        shards, mesh=mesh, in_specs=placed, out_specs=P("rows", "cols"), check_vma=False
    )
```

profile of v0, /device:TPU:16, one launch (start us, length us, event | category | flops | bytes accessed | tf_op | source)
XLA Modules:
  0.0 754.6 jit_solution(9624634156711667488)
XLA Ops:
  0.0 1.6 fusion.10
  1.6 1.5 fusion.11
  3.1 1.3 collective-permute-start.1
  4.4 4.1 collective-permute-start
  8.5 0.0 copy-done
  8.5 1.3 collective-permute-start.5
  9.8 3.8 collective-permute-start.4
  13.6 0.0 copy-done.1
  13.6 0.1 copy.5
  13.7 0.1 compare_reduce_fusion
  13.8 0.1 copy.6
  13.9 6.2 mul.127
  20.1 12.3 %copy.8 = f32[384,8,4,256]{3,1,2,0:T(8,128)} copy(f32[384,8,4,256]{3,2,1,0:T(4,128)} %bitcast.18) | data formatting | bytes 25165824
  32.4 12.6 %copy.7 = f32[1024,3072]{1,0:T(8,128)} copy(f32[1024,3072]{0,1:T(8,128)} %bitcast.19) | data formatting | bytes 25165824 | tf_op jit(solution)/shard_map/mul | solution.py:60
  45.0 0.0 collective-permute-done.1
  45.0 0.0 collective-permute-done
  45.0 1.4 pad_maximum_fusion
  46.4 9.5 %fusion.20 = (f32[1024]{0:T(1024)S(1)}, f32[1024,3072]{1,0:T(8,128)}) fusion(f32[1024,3072]{1,0:T(8,128)} %copy.7, bf16[1024,512]{1,0:T(8,128)(2,1)S(1)} %fusion.11, bf16[3072,512]{1,0:T(8,128)(2,1)S(1)} %bitcast.29), kind=kOutput, calls=%fused_computation.42 | convolution fusion | flops 3236953088 | bytes 29364224 | tf_op jit(solution)/shard_map/dot_general | solution.py:47
  55.9 1.3 collective-permute-start.3
  57.2 3.2 collective-permute-start.2
  60.5 0.0 collective-permute-done.5
  60.5 0.0 collective-permute-done.4
  60.5 1.1 pad_maximum_fusion.1
  61.7 0.0 collective-permute-done.3
  61.7 0.0 collective-permute-done.2
  61.7 13.3 %multiply_reduce_fusion.3 = (f32[128]{0:T(128)S(1)}, f32[128]{0:T(128)S(1)}, f32[1024,128]{1,0:T(8,128)S(1)}) fusion(f32[1024,128]{1,0:T(8,128)S(1)} %copy-done, f32[3072,128]{1,0:T(8,128)S(1)} %bitcast.33, f32[1024,3072]{1,0:T(8,128)} %get-tuple-element.12, f32[3072]{0:T(1024)S(1)} %mul.132, f32[1024]{0:T(1024)S(1)} %rsqrt.20), kind=kOutput, calls=%fused_computation.36 | convolution fusion | flops 4838916096 | bytes 15221760 | tf_op jit(solution)/shard_map/dot_general | solution.py:75
  75.0 131.9 %all-reduce = (f32[128]{0:T(128)S(1)}, f32[128]{0:T(128)S(1)}) all-reduce(f32[128]{0:T(128)S(1)} %get-tuple-element.6, f32[128]{0:T(128)S(1)} %get-tuple-element.5), channel_id=1, replica_groups=mesh['rows'=64,'cols'=4] {'rows'}, use_global_device_ids=true, to_apply=%region_1.0 | all-reduce | flops 256 | bytes 2048 | tf_op jit(solution)/shard_map/psum | solution.py:33
  206.9 0.2 multiply_reduce_fusion.2
  207.0 124.0 %psum.44 = f32[128]{0:T(128)S(1)} all-reduce(f32[128]{0:T(128)S(1)} %get-tuple-element.9), channel_id=1, replica_groups=mesh['rows'=64,'cols'=4] {'rows'}, use_global_device_ids=true, to_apply=%region_8.0 | all-reduce | flops 128 | bytes 1024 | tf_op jit(solution)/shard_map/psum | solution.py:33
  331.1 0.1 multiply_add_fusion.2
  331.2 1.3 collective-permute-start.7
  332.5 3.1 collective-permute-start.6
  335.5 0.0 collective-permute-done.7
  335.5 1.5 collective-permute-done.6
  337.0 0.1 pad_maximum_fusion.2
  337.1 13.3 %multiply_reduce_fusion.1 = (f32[128]{0:T(128)S(1)}, f32[1024,128]{1,0:T(8,128)S(1)}) fusion(f32[1024,128]{1,0:T(8,128)S(1)} %multiply_add_fusion.2, f32[3072,128]{1,0:T(8,128)S(1)} %bitcast.35, f32[1024,3072]{1,0:T(8,128)} %get-tuple-element.12, f32[3072]{0:T(1024)S(1)} %mul.132, f32[1024]{0:T(1024)S(1)} %rsqrt.20), kind=kOutput, calls=%fused_computation.32 | convolution fusion | flops 4838653952 | bytes 15221248 | tf_op jit(solution)/shard_map/dot_general | solution.py:75
  350.5 130.0 %psum.45 = f32[128]{0:T(128)S(1)} all-reduce(f32[128]{0:T(128)S(1)} %get-tuple-element.14), channel_id=1, replica_groups=mesh['rows'=64,'cols'=4] {'rows'}, use_global_device_ids=true, to_apply=%region_10.0 | all-reduce | flops 128 | bytes 1024 | tf_op jit(solution)/shard_map/psum | solution.py:82
  480.4 0.2 multiply_reduce_fusion
  480.6 124.0 %psum.46 = f32[128]{0:T(128)S(1)} all-reduce(f32[128]{0:T(128)S(1)} %multiply_reduce_fusion), channel_id=1, replica_groups=mesh['rows'=64,'cols'=4] {'rows'}, use_global_device_ids=true, to_apply=%region_12.0 | all-reduce | flops 128 | bytes 1024 | tf_op jit(solution)/shard_map/psum | solution.py:33
  604.7 0.1 multiply_add_fusion.1
  604.7 1.3 collective-permute-start.9
  606.0 3.1 collective-permute-start.8
  609.1 0.0 collective-permute-done.9
  609.1 1.5 collective-permute-done.8
  610.6 0.1 pad_maximum_fusion.3
  610.7 13.2 %fusion.19 = f32[128]{0:T(128)S(1)} fusion(f32[1024,128]{1,0:T(8,128)S(1)} %multiply_add_fusion.1, f32[3072,128]{1,0:T(8,128)S(1)} %bitcast.34, f32[1024,3072]{1,0:T(8,128)} %get-tuple-element.12, f32[3072]{0:T(1024)S(1)} %mul.132, f32[1024]{0:T(1024)S(1)} %rsqrt.20), kind=kOutput, calls=%fused_computation.27 | convolution fusion | flops 4838653952 | bytes 14696960 | tf_op jit(solution)/shard_map/dot_general | solution.py:75
  624.0 129.7 %psum.47 = f32[128]{0:T(128)S(1)} all-reduce(f32[128]{0:T(128)S(1)} %fusion.19), channel_id=1, replica_groups=mesh['rows'=64,'cols'=4] {'rows'}, use_global_device_ids=true, to_apply=%region_14.0 | all-reduce | flops 128 | bytes 1024 | tf_op jit(solution)/shard_map/psum | solution.py:82
  753.7 0.9 multiply_add_fusion
  (14 shorter events, 0.1 us)
Async XLA Ops:
  0.0 8.5 %copy-start = (f32[1024,128]{1,0:T(8,128)S(1)}, f32[1024,128]{1,0:T(8,128)}, u32[]{:S(2)}) copy-start(f32[1024,128]{1,0:T(8,128)} %param.5) | copy-start | bytes 1572868
  0.0 13.6 %copy-start.1 = (s32[4,12]{1,0:T(4,128)S(1)}, s32[4,12]{1,0:T(4,128)}, u32[]{:S(2)}) copy-start(s32[4,12]{1,0:T(4,128)} %param.4) | copy-start | bytes 580
  3.1 41.9 %collective-permute-start.1 = (bf16[4,256,512]{2,1,0:T(8,128)(2,1)S(1)}, bf16[4,256,512]{2,1,0:T(8,128)(2,1)S(1)}, u32[]{:S(2)}, u32[]{:S(2)}) collective-permute-start(bf16[4,256,512]{2,1,0:T(8,128)(2,1)S(1)} %bitcast.26), channel_id=1, source_target_pairs={{4,0},{8,4},{12,8},{16,12},{20,16},{24,20},{28,24},{32,28},{36,32}... | collective-permute-start | bytes 3145736 | tf_op jit(solution)/shard_map/ppermute | solution.py:23
  4.4 40.6 %collective-permute-start = (bf16[4,256,512]{2,1,0:T(8,128)(2,1)S(1)}, bf16[4,256,512]{2,1,0:T(8,128)(2,1)}, u32[]{:S(2)}, u32[]{:S(2)}) collective-permute-start(bf16[4,256,512]{2,1,0:T(8,128)(2,1)S(1)} %bitcast.27), channel_id=1, source_target_pairs={{0,4},{4,8},{8,12},{12,16},{16,20},{20,24},{24,28},{28,32},{32,36}... | collective-permute-start | bytes 3145736 | tf_op jit(solution)/shard_map/ppermute | solution.py:22
  8.5 52.0 %collective-permute-start.5 = (f32[4,256,128]{2,1,0:T(8,128)S(1)}, f32[4,256,128]{2,1,0:T(8,128)S(1)}, u32[]{:S(2)}, u32[]{:S(2)}) collective-permute-start(f32[4,256,128]{2,1,0:T(8,128)S(1)} %bitcast.20), channel_id=1, source_target_pairs={{4,0},{8,4},{12,8},{16,12},{20,16},{24,20},{28,24},{32,28},{36,32}... | collective-permute-start | bytes 1572872 | tf_op jit(solution)/shard_map/ppermute | solution.py:23
  9.8 50.7 %collective-permute-start.4 = (f32[4,256,128]{2,1,0:T(8,128)S(1)}, f32[4,256,128]{2,1,0:T(8,128)}, u32[]{:S(2)}, u32[]{:S(2)}) collective-permute-start(f32[4,256,128]{2,1,0:T(8,128)S(1)} %bitcast.21), channel_id=1, source_target_pairs={{0,4},{4,8},{8,12},{12,16},{16,20},{20,24},{24,28},{28,32},{32,36}... | collective-permute-start | bytes 1572872 | tf_op jit(solution)/shard_map/ppermute | solution.py:22
  55.9 5.7 collective-permute-start.3
  57.2 4.4 collective-permute-start.2
  331.2 4.4 collective-permute-start.7
  332.5 4.6 collective-permute-start.6
  604.7 4.4 collective-permute-start.9
  606.0 4.6 collective-permute-start.8
where the time goes:
time: 770 us; the launch traced here: 755 us
  blocking collectives  640 us (83%)
  matrix products  49.4 us (6%)
  local copies, waits for them, and re-layouts  31.3 us (4%)
  starting transfers between devices  23.7 us (3%)
    psum x3, blocking collectives, squares(): return lax.psum(column_sums(residual, residual), 'rows')  380 us
    psum x2, blocking collectives, shards(): curvature = lax.psum(column_sums(direction, image), 'rows')  260 us
    dot_general x3, matrix products, shards(): jnp.dot(banded, nearby.reshape(3 * own_rows, columns), precision=highest,...  39.9 us
    mul x2, local copies, waits for them, and re-layouts, shards(): cubed.reshape(own_blocks, block_rows, 3 * own_blocks, block_rows)  18.8 us
    ppermute x5, starting transfers between devices, extended(): before = lax.ppermute(last, axis, up)  17.3 us
  transfers between devices with their start and end apart: 10, of which 2 were waited for; matrix products, arithmetic and copies ran while one was open for 6% of the time, Pallas kernels for 0%

commit v1 on v0

v1 whole, which is shorter than its diff:
```python
import math

import jax
import jax.numpy as jnp
from jax import lax
from jax.experimental import pallas as pl
from jax.experimental.pallas import tpu as pltpu
from jax.sharding import Mesh, PartitionSpec as P

diffusion = 0.9
epsilon = 1e-06
tiny = 2e-07
f32 = jnp.float32
bf16 = jnp.bfloat16
ROWS = ("z", "x", "core")


def unit_rows(raw):
    values = raw.astype(f32)
    total = jnp.sum(values * values, axis=1, keepdims=True)
    return (values * lax.rsqrt(total + epsilon)).astype(bf16)


def affinity_kernel(linked, own_ref, other_ref, w_ref, deg_ref, unit_ref):
    step = pl.program_id(0)
    blocks = linked.shape[0]
    rows = own_ref.shape[0] // blocks

    @pl.when(step == 0)
    def _():
        unit_ref[...] = unit_rows(own_ref[...])
        deg_ref[...] = jnp.zeros_like(deg_ref)

    other = unit_rows(other_ref[...])
    for b in range(blocks):
        part = pl.ds(b * rows, rows)
        similar = lax.dot_general(
            unit_ref[part, :], other, (((1,), (1,)), ((), ())), preferred_element_type=f32
        )
        kept = jnp.maximum(similar, 0.0)
        w = kept * kept * (kept * linked[b, step])
        high = w.astype(bf16)
        w_ref[pl.ds(2 * b * rows, rows), :] = high
        w_ref[pl.ds((2 * b + 1) * rows, rows), :] = (w - high.astype(f32)).astype(bf16)
        half = w.shape[1] // 2
        deg_ref[part, :] += w[:, :half] + w[:, half:]


def affinity(own, other, linked):
    n, features = own.shape
    blocks = linked.shape[0]
    rows = n // blocks
    return pl.pallas_call(
        affinity_kernel,
        grid_spec=pltpu.PrefetchScalarGridSpec(
            num_scalar_prefetch=1,
            grid=(blocks,),
            in_specs=[
                pl.BlockSpec((n, features), lambda c, m: (0, 0)),
                pl.BlockSpec((rows, features), lambda c, m: (c, 0)),
            ],
            out_specs=[
                pl.BlockSpec((2 * n, rows), lambda c, m: (0, c)),
                pl.BlockSpec((n, 128), lambda c, m: (0, 0)),
            ],
            scratch_shapes=[pltpu.VMEM((n, features), bf16)],
        ),
        out_shape=[
            jax.ShapeDtypeStruct((2 * n, n), bf16),
            jax.ShapeDtypeStruct((n, 128), f32),
        ],
        cost_estimate=pl.CostEstimate(flops=2 * n * n * features, bytes_accessed=8 * n * n, transcendentals=0),
        compiler_params=pltpu.CompilerParams(vmem_limit_bytes=32 << 20),
    )(linked, own, other)


def product_kernel(w_ref, u_ref, base_ref, out_ref):
    rows, columns = out_ref.shape
    wide = jnp.dot(w_ref[...], u_ref[...], preferred_element_type=f32)
    both = wide[:rows] + wide[rows:]
    out_ref[...] = base_ref[...] + (both[:, :columns] + both[:, columns:])


def product(w, split, base):
    n, columns = base.shape
    rows = n // 4
    return pl.pallas_call(
        product_kernel,
        grid=(4,),
        in_specs=[
            pl.BlockSpec((2 * rows, n), lambda b: (b, 0)),
            pl.BlockSpec((n, 2 * columns), lambda b: (0, 0)),
            pl.BlockSpec((rows, columns), lambda b: (b, 0)),
        ],
        out_specs=pl.BlockSpec((rows, columns), lambda b: (b, 0)),
        out_shape=jax.ShapeDtypeStruct((n, columns), f32),
        cost_estimate=pl.CostEstimate(flops=8 * n * n * columns, bytes_accessed=4 * n * n, transcendentals=0),
        compiler_params=pltpu.CompilerParams(vmem_limit_bytes=32 << 20),
    )(w, split, base)


def split(values):
    high = lax.reduce_precision(values, 8, 7)
    return jnp.concatenate([high.astype(bf16), (values - high).astype(bf16)], axis=1)


def exchanges():
    peers = math.prod(lax.axis_size(axis) for axis in ROWS)
    up = [(i, i + 1) for i in range(1, peers - 1, 2)]
    pairs = up + [(j, i) for i, j in up]

    def outer(array):
        return lax.ppermute(array, ROWS, pairs)

    return outer, swap


def swap(array):
    return lax.ppermute(array, "core", [(0, 1), (1, 0)])


def gathered(part):
    copies = jnp.broadcast_to(part[None], (32,) + part.shape)
    return lax.all_to_all(copies, ("z", "x"), 0, 0)


def moments(parts):
    b00, b01, b02, b03, b11, b12, b13, b22, b23, own = [parts[:, k] for k in range(10)]
    mass = jnp.sum(b00, axis=0)
    shift = jnp.sum(own * b00 + b01, axis=0) / mass
    d = own - shift[None]
    m1 = b01 + d * b00
    m2 = b11 + d * (2 * b01 + d * b00)
    m3 = b12 + d * (2 * b11 + b02 + d * (3 * b01 + d * b00))
    m4 = b22 + d * (4 * b12 + d * (2 * b02 + 4 * b11 + d * (4 * b01 + d * b00)))
    m5 = b23 + d * (
        3 * b22 + 2 * b13 + d * (9 * b12 + b03 + d * (4 * b02 + 6 * b11 + d * (5 * b01 + d * b00)))
    )
    return shift, [mass] + [jnp.sum(m, axis=0) for m in (m1, m2, m3, m4, m5)]


def coefficients(shift, m):
    level = 1.0 - diffusion * shift
    h = [level * m[k] - diffusion * m[k + 1] for k in range(5)]
    least, most = 1.0 / (1.0 + diffusion), 1.0 / (1.0 - diffusion)
    l10 = h[1] / h[0]
    l20 = h[2] / h[0]
    d1 = jnp.maximum(h[2] - l10 * h[1], tiny * h[2])
    e21 = h[3] - l20 * h[1]
    l21 = e21 / d1
    d2 = jnp.maximum(h[4] - l20 * h[2] - l21 * e21, tiny * h[4])
    b0 = m[0]
    b1 = m[1] - l10 * b0
    b2 = m[2] - l20 * b0 - l21 * b1
    y0 = b0 / h[0]
    y1 = diffusion * y0 * jnp.clip(b1 / (d1 * diffusion * y0), least, most)
    y2 = diffusion * y1 * jnp.clip(b2 / (d2 * diffusion * y1), least, most)
    c2 = y2
    c1 = y1 - l21 * c2
    c0 = y0 - l10 * c1 - l20 * c2
    return c0, c1, c2


def powers(shift, g0, g1, g2):
    v1 = g1 - shift * g0
    t1 = g2 - shift * g1
    return v1, t1, t1 - shift * v1


def dots(pairs):
    return jnp.stack([jnp.sum(a * b, axis=0) for a, b in pairs])


def shards(embeddings, neighbours, queries):
    outer, inner = exchanges()
    blocks = neighbours.shape[0]
    index = lax.axis_index(ROWS)
    core = lax.axis_index("core")
    e_out, e_in = outer(embeddings), inner(embeddings)
    q_out, q_in = outer(queries), inner(queries)
    owners = jnp.stack([index, index + 1 - 2 * core, index - 1 + 2 * core])
    candidates = owners[:, None] * blocks + jnp.arange(blocks, dtype=jnp.int32)
    linked = jnp.any(neighbours[None, :, None, :] == candidates[:, None, :, None], axis=3).astype(f32)

    w_own, deg_own = affinity(embeddings, embeddings, linked[0])
    w_in, deg_in = affinity(embeddings, e_in, linked[1])
    w_out, deg_out = affinity(embeddings, e_out, linked[2])
    scale = lax.rsqrt(jnp.sum(deg_own + deg_in + deg_out, axis=1))
    s_out, s_in = outer(scale), inner(scale)
    zero = jnp.zeros_like(queries)
    column = scale[:, None]

    def apply(own, near, far):
        mixed = product(w_own, own, zero)
        mixed = product(w_in, near, mixed)
        return column * product(w_out, far, mixed)

    g0 = queries
    g1 = apply(split(column * g0), split(s_in[:, None] * q_in), split(s_out[:, None] * q_out))
    u1 = split(column * g1)
    u1_out, u1_in = outer(u1), inner(u1)
    early = dots(((g0, g0), (g0, g1)))
    early = early + inner(early)
    own_shift = jnp.clip(jnp.where(early[0] > 0, early[1] / early[0], 0.0), -1.0, 1.0)
    g2 = apply(u1, u1_in, u1_out)
    u2 = split(column * g2)
    u2_out, u2_in = outer(u2), inner(u2)
    g3 = apply(u2, u2_in, u2_out)
    v1, t1, v2 = powers(own_shift, g0, g1, g2)
    v3 = (g3 - own_shift * g2) - own_shift * t1 - own_shift * v2
    part = dots(
        ((g0, g0), (g0, v1), (g0, v2), (g0, v3), (v1, v1), (v1, v2), (v1, v3), (v2, v2), (v2, v3))
    )
    part = part + inner(part)
    shift, m = moments(gathered(jnp.concatenate([part, own_shift[None]])))
    c0, c1, c2 = coefficients(shift, m)
    v1, _, v2 = powers(shift, g0, g1, g2)
    return c0 * g0 + c1 * v1 + c2 * v2


def solution(mesh):
    fine = Mesh(mesh.devices.reshape(8, 4, 2, 4), ("z", "x", "core", "cols"))
    placed = (P(ROWS, None), P(ROWS, None), P(ROWS, "cols"))
    return jax.shard_map(
        shards, mesh=fine, in_specs=placed, out_specs=P(ROWS, "cols"), check_vma=False
    )
```

time: 770 us -> 94.1 us (0.12); the launches traced: 755 us -> 93.7 us
  blocking collectives: 640 us -> 31.5 us
  matrix products: 49.4 us -> 0 us
  local copies, waits for them, and re-layouts: 31.3 us -> 1.44 us
  Pallas kernels: 0 us -> 28.5 us
    psum x5 -> x0, blocking collectives: 640 us -> none  [the longest x3 380 us: squares(): return lax.psum(column_sums(residual, residual), 'rows')]
    dot_general x4 -> x0, matrix products: 49.4 us -> none  [the longest x3 39.9 us: shards(): jnp.dot(banded, nearby.reshape(3 * own_rows, columns), precision=highest,...]
    all_to_all x0 -> x1, blocking collectives: none -> 31.5 us  [gathered(): return lax.all_to_all(copies, ('z', 'x'), 0, 0)]
    pallas_call x0 -> x12, Pallas kernels: none -> 28.5 us  [the longest x9 16 us: product(): pl.pallas_call(product_kernel, grid=(4,), in_specs=[pl.BlockSpec((2 * row...]
    mul x3 -> x0, local copies, waits for them, and re-layouts: 18.8 us -> none  [the longest x2 18.8 us: shards(): cubed.reshape(own_blocks, block_rows, 3 * own_blocks, block_rows)]
    unnamed x6 -> x4, local copies, waits for them, and re-layouts: 12.4 us -> 1.23 us
    ppermute x10 -> x12, starting transfers between devices: 23.7 us -> 25.3 us  [the longest x7 21.9 us: swap(): return lax.ppermute(array, 'core', [(0, 1), (1, 0)])]
  transfers between devices with their start and end apart: 10 -> 12, of which waited for: 2 -> 1; matrix products, arithmetic and copies ran while one was open for 6% -> 4% of each run, Pallas kernels for 0% -> 25%
where the time goes in v1:
time: 94.1 us; the launch traced here: 93.7 us
  blocking collectives  31.5 us (33%)
  Pallas kernels  28.5 us (30%)
  starting transfers between devices  25.3 us (27%)
  other arithmetic  5.73 us (6%)
  local copies, waits for them, and re-layouts  1.44 us (2%)
    all_to_all x1, blocking collectives, gathered(): return lax.all_to_all(copies, ('z', 'x'), 0, 0)  31.5 us
    ppermute x7, starting transfers between devices, swap(): return lax.ppermute(array, 'core', [(0, 1), (1, 0)])  21.9 us
    pallas_call x9, Pallas kernels, product(): pl.pallas_call(product_kernel, grid=(4,), in_specs=[pl.BlockSpec((2 * row...  16 us
    pallas_call x3, Pallas kernels, affinity(): pl.pallas_call(affinity_kernel, grid_spec=pltpu.PrefetchScalarGridSpec(nu...  12.5 us
    ppermute x5, starting transfers between devices, outer(): return lax.ppermute(array, ROWS, pairs)  3.41 us
  transfers between devices with their start and end apart: 12, of which 1 were waited for; matrix products, arithmetic and copies ran while one was open for 4% of the time, Pallas kernels for 25%

profile of v1, /device:TPU:16, one launch (start us, length us, event | category | flops | bytes accessed | tf_op | source)
XLA Modules:
  0.0 93.7 jit_solution(8478748455127595493)
XLA Ops:
  0.0 0.0 collective-permute-start
  0.0 0.7 collective-permute-start.1
  0.7 2.9 %collective-permute-start.5 = (f32[1024,128]{1,0:T(8,128)}, f32[1024,128]{1,0:T(8,128)}, u32[]{:S(2)}, u32[]{:S(2)}) collective-permute-start(f32[1024,128]{1,0:T(8,128)} %param.5), channel_id=1, source_target_pairs={{0,4},{4,0},{1,5},{5,1},{2,6},{6,2},{3,7},{7,3},{8,12},{12,8},{9,1... | collective-permute-start | bytes 1572872 | tf_op jit(solution)/shard_map/ppermute | solution.py:119
  3.6 0.7 collective-permute-start.3
  4.3 0.1 add_multiply_fusion
  4.4 0.1 iota_add_fusion
  4.5 1.0 %compare_reduce_fusion = pred[3,4,4]{2,1,0:T(4,128)(4,1)S(1)} fusion(s32[3,4]{1,0:T(4,128)S(1)} %iota_add_fusion, s32[4,12]{1,0:T(4,128)} %param.4), kind=kLoop, calls=%fused_computation.36 | loop fusion | flops 1104 | bytes 288 | tf_op jit(solution)/shard_map/reduce_or | solution.py:183
  5.5 0.0 copy-start
  5.5 1.2 %copy-done = bf16[1024,512]{1,0:T(8,128)(2,1)S(1)} copy-done((bf16[1024,512]{1,0:T(8,128)(2,1)S(1)}, bf16[1024,512]{1,0:T(8,128)(2,1)}, u32[]{:S(2)}) %copy-start) | copy-done | bytes 1048600
  6.7 4.2 %shard_map.37 = (bf16[2048,1024]{1,0:T(8,128)(2,1)S(1)}, f32[1024,128]{1,0:T(8,128)S(1)}) custom-call(f32[4,4]{1,0:T(4,128)S(1)} %get-tuple-element.66.linked, bf16[1024,512]{1,0:T(8,128)(2,1)S(1)} %copy-done, bf16[1024,512]{1,0:T(8,128)(2,1)S(1)} %copy-done), custom_call_target="tpu_custom_call" | custom-call | flops 1073741824 | bytes 8388608 | tf_op jit(solution)/shard_map/pallas_call | solution.py:53
  10.9 0.0 copy-start.1
  10.9 4.2 %shard_map.38 = (bf16[2048,1024]{1,0:T(8,128)(2,1)S(1)}, f32[1024,128]{1,0:T(8,128)S(1)}) custom-call(f32[4,4]{1,0:T(4,128)S(1)} %get-tuple-element.64.linked, bf16[1024,512]{1,0:T(8,128)(2,1)S(1)} %copy-done, bf16[1024,512]{1,0:T(8,128)(2,1)S(1)} %collective-permute-done.other_ref), custom_call_target="tpu_custom_call" | custom-call | flops 1073741824 | bytes 8388608 | tf_op jit(solution)/shard_map/pallas_call | solution.py:53
  15.1 4.2 %shard_map.39 = (bf16[2048,1024]{1,0:T(8,128)(2,1)S(1)}, f32[1024,128]{1,0:T(8,128)S(1)}) custom-call(f32[4,4]{1,0:T(4,128)S(1)} %get-tuple-element.65.linked, bf16[1024,512]{1,0:T(8,128)(2,1)S(1)} %copy-done, bf16[1024,512]{1,0:T(8,128)(2,1)S(1)} %collective-permute-done.1.other_ref), custom_call_target="tpu_custom_call" | custom-call | flops 1073741824 | bytes 8388608 | tf_op jit(solution)/shard_map/pallas_call | solution.py:53
  19.3 0.2 add_reduce_fusion
  19.5 2.9 %collective-permute-start.4 = (f32[1024]{0:T(1024)S(1)}, f32[1024]{0:T(1024)S(1)}, u32[]{:S(2)}, u32[]{:S(2)}) collective-permute-start(f32[1024]{0:T(1024)S(1)} %rsqrt.7), channel_id=1, source_target_pairs={{0,4},{4,0},{1,5},{5,1},{2,6},{6,2},{3,7},{7,3},{8,12},{12,8},{9,1... | collective-permute-start | bytes 12296 | tf_op jit(solution)/shard_map/ppermute | solution.py:119
  22.5 0.6 collective-permute-start.2
  23.2 0.2 reduce-precision_convert_fusion.2
  23.4 0.1 pad_maximum_fusion.2.u_ref
  23.5 1.8 %shard_map.40.base_ref = f32[1024,128]{1,0:T(8,128)S(1)} custom-call(bf16[2048,1024]{1,0:T(8,128)(2,1)S(1)} %get-tuple-element.16.w_ref, bf16[1024,256]{1,0:T(8,128)(2,1)S(1)} %pad_maximum_fusion.2.u_ref, f32[1024,128]{1,0:T(8,128)S(1)} %broadcast_in_dim.5.base_ref), custom_call_target="tpu_custom_call" | custom-call | flops 1073741824 | bytes 4194304 | tf_op jit(solution)/shard_map/pallas_call | solution.py:87
  25.3 1.2 %reduce-precision_convert_fusion.3 = (bf16[1024,128]{1,0:T(8,128)(2,1)S(1)}, bf16[1024,128]{1,0:T(8,128)(2,1)S(1)}) fusion(f32[1024,128]{1,0:T(8,128)} %collective-permute-done.5, f32[1024]{0:T(1024)S(1)} %collective-permute-done.4), kind=kLoop, calls=%fused_computation.7 | loop fusion | flops 655360 | bytes 1052672 | tf_op jit(solution)/shard_map/convert_element_type | solution.py:104
  26.5 0.1 pad_maximum_fusion.1.u_ref
  26.6 0.2 reduce-precision_convert_fusion.4
  26.8 0.1 pad_maximum_fusion.u_ref
  26.9 1.8 %shard_map.41.base_ref = f32[1024,128]{1,0:T(8,128)S(1)} custom-call(bf16[2048,1024]{1,0:T(8,128)(2,1)S(1)} %get-tuple-element.15.w_ref, bf16[1024,256]{1,0:T(8,128)(2,1)S(1)} %pad_maximum_fusion.1.u_ref, f32[1024,128]{1,0:T(8,128)S(1)} %shard_map.40.base_ref), custom_call_target="tpu_custom_call" | custom-call | flops 1073741824 | bytes 4194304 | tf_op jit(solution)/shard_map/pallas_call | solution.py:87
  28.7 1.8 %shard_map.42 = f32[1024,128]{1,0:T(8,128)S(1)} custom-call(bf16[2048,1024]{1,0:T(8,128)(2,1)S(1)} %get-tuple-element.14.w_ref, bf16[1024,256]{1,0:T(8,128)(2,1)S(1)} %pad_maximum_fusion.u_ref, f32[1024,128]{1,0:T(8,128)S(1)} %shard_map.41.base_ref), custom_call_target="tpu_custom_call" | custom-call | flops 1073741824 | bytes 4194304 | tf_op jit(solution)/shard_map/pallas_call | solution.py:87
  30.5 0.2 multiply_reduce_fusion.9
  30.7 0.1 pad_maximum_fusion.3.u_ref
  30.8 2.6 %collective-permute-start.8 = (bf16[1024,256]{1,0:T(8,128)(2,1)S(1)}, bf16[1024,256]{1,0:T(8,128)(2,1)S(1)}, u32[]{:S(2)}, u32[]{:S(2)}) collective-permute-start(bf16[1024,256]{1,0:T(8,128)(2,1)S(1)} %pad_maximum_fusion.3.u_ref), channel_id=1, source_target_pairs={{0,4},{4,0},{1,5},{5,1},{2,6},{6,2},{3,7},{7,3},{8,12},{12,8},{9,1... | collective-permute-start | bytes 1572872 | tf_op jit(solution)/shard_map/ppermute | solution.py:119
  33.4 0.7 collective-permute-start.7
  34.1 3.3 %collective-permute-start.6 = (f32[2,128]{1,0:T(2,128)S(1)}, f32[2,128]{1,0:T(2,128)S(1)}, u32[]{:S(2)}, u32[]{:S(2)}) collective-permute-start(f32[2,128]{1,0:T(2,128)S(1)} %pad_maximum_fusion.6), channel_id=1, source_target_pairs={{0,4},{4,0},{1,5},{5,1},{2,6},{6,2},{3,7},{7,3},{8,12},{12,8},{9,1... | collective-permute-start | bytes 3080 | tf_op jit(solution)/shard_map/ppermute | solution.py:119
  37.4 1.8 %shard_map.43.base_ref = f32[1024,128]{1,0:T(8,128)S(1)} custom-call(bf16[2048,1024]{1,0:T(8,128)(2,1)S(1)} %get-tuple-element.16.w_ref, bf16[1024,256]{1,0:T(8,128)(2,1)S(1)} %pad_maximum_fusion.3.u_ref, f32[1024,128]{1,0:T(8,128)S(1)} %broadcast_in_dim.5.base_ref), custom_call_target="tpu_custom_call" | custom-call | flops 1073741824 | bytes 4194304 | tf_op jit(solution)/shard_map/pallas_call | solution.py:87
  39.2 1.8 %shard_map.44.base_ref = f32[1024,128]{1,0:T(8,128)S(1)} custom-call(bf16[2048,1024]{1,0:T(8,128)(2,1)S(1)} %get-tuple-element.15.w_ref, bf16[1024,256]{1,0:T(8,128)(2,1)S(1)} %collective-permute-done.8.u_ref, f32[1024,128]{1,0:T(8,128)S(1)} %shard_map.43.base_ref), custom_call_target="tpu_custom_call" | custom-call | flops 1073741824 | bytes 4194304 | tf_op jit(solution)/shard_map/pallas_call | solution.py:87
  41.0 1.8 %shard_map.45 = f32[1024,128]{1,0:T(8,128)S(1)} custom-call(bf16[2048,1024]{1,0:T(8,128)(2,1)S(1)} %get-tuple-element.14.w_ref, bf16[1024,256]{1,0:T(8,128)(2,1)S(1)} %collective-permute-done.7.u_ref, f32[1024,128]{1,0:T(8,128)S(1)} %shard_map.44.base_ref), custom_call_target="tpu_custom_call" | custom-call | flops 1073741824 | bytes 4194304 | tf_op jit(solution)/shard_map/pallas_call | solution.py:87
  42.7 0.2 reduce-precision_convert_fusion
  42.9 0.1 pad_maximum_fusion.4.u_ref
  43.0 3.2 %collective-permute-start.10 = (bf16[1024,256]{1,0:T(8,128)(2,1)S(1)}, bf16[1024,256]{1,0:T(8,128)(2,1)S(1)}, u32[]{:S(2)}, u32[]{:S(2)}) collective-permute-start(bf16[1024,256]{1,0:T(8,128)(2,1)S(1)} %pad_maximum_fusion.4.u_ref), channel_id=1, source_target_pairs={{0,4},{4,0},{1,5},{5,1},{2,6},{6,2},{3,7},{7,3},{8,12},{12,8},{9,1... | collective-permute-start | bytes 1572872 | tf_op jit(solution)/shard_map/ppermute | solution.py:119
  46.3 0.7 collective-permute-start.9
  47.0 1.8 %shard_map.46.base_ref = f32[1024,128]{1,0:T(8,128)S(1)} custom-call(bf16[2048,1024]{1,0:T(8,128)(2,1)S(1)} %get-tuple-element.16.w_ref, bf16[1024,256]{1,0:T(8,128)(2,1)S(1)} %pad_maximum_fusion.4.u_ref, f32[1024,128]{1,0:T(8,128)S(1)} %broadcast_in_dim.5.base_ref), custom_call_target="tpu_custom_call" | custom-call | flops 1073741824 | bytes 4194304 | tf_op jit(solution)/shard_map/pallas_call | solution.py:87
  48.8 1.8 %shard_map.47.base_ref = f32[1024,128]{1,0:T(8,128)S(1)} custom-call(bf16[2048,1024]{1,0:T(8,128)(2,1)S(1)} %get-tuple-element.15.w_ref, bf16[1024,256]{1,0:T(8,128)(2,1)S(1)} %collective-permute-done.10.u_ref, f32[1024,128]{1,0:T(8,128)S(1)} %shard_map.46.base_ref), custom_call_target="tpu_custom_call" | custom-call | flops 1073741824 | bytes 4194304 | tf_op jit(solution)/shard_map/pallas_call | solution.py:87
  50.6 1.8 %shard_map.48 = f32[1024,128]{1,0:T(8,128)S(1)} custom-call(bf16[2048,1024]{1,0:T(8,128)(2,1)S(1)} %get-tuple-element.14.w_ref, bf16[1024,256]{1,0:T(8,128)(2,1)S(1)} %collective-permute-done.9.u_ref, f32[1024,128]{1,0:T(8,128)S(1)} %shard_map.47.base_ref), custom_call_target="tpu_custom_call" | custom-call | flops 1073741824 | bytes 4194304 | tf_op jit(solution)/shard_map/pallas_call | solution.py:87
  52.4 0.3 multiply_subtract_fusion
  52.7 0.3 multiply_reduce_fusion
  53.0 6.9 %collective-permute-start.11 = (f32[9,128]{1,0:T(8,128)S(1)}, f32[9,128]{1,0:T(8,128)S(1)}, u32[]{:S(2)}, u32[]{:S(2)}) collective-permute-start(f32[9,128]{1,0:T(8,128)S(1)} %stack.64), channel_id=1, source_target_pairs={{0,4},{4,0},{1,5},{5,1},{2,6},{6,2},{3,7},{7,3},{8,12},{12,8},{9,1... | collective-permute-start | bytes 13832 | tf_op jit(solution)/shard_map/ppermute | solution.py:119
  60.0 0.8 collective-permute-done.11
  60.8 31.5 %all_to_all.5 = f32[32,10,128]{2,1,0:T(8,128)S(1)} all-to-all(f32[32,10,128]{2,1,0:T(8,128)S(1)} %broadcast_in_dim.6), channel_id=1, replica_groups=mesh['z'=8,'x'=4,'core'=2,'cols'=4] {'z','x'}, dimensions={0} | all-to-all | bytes 327680 | tf_op jit(solution)/shard_map/all_to_all | solution.py:124
  92.3 0.1 fusion.16
  92.5 0.1 fusion.8
  92.6 1.1 %multiply_add_fusion = f32[1024,128]{1,0:T(8,128)} fusion(f32[1024,128]{1,0:T(8,128)S(1)} %copy-done.1, f32[1024,128]{1,0:T(8,128)S(1)} %shard_map.45, f32[1024,128]{1,0:T(8,128)S(1)} %shard_map.42, f32[128]{0:T(128)S(1)} %get-tuple-element.34, f32[128]{0:T(128)S(1)} %div.99, f32[128]{0:T(128)S(1)} %get-tuple-element.33, f32[128]{0:T(128)S(1)} %get-tuple-element.32, ...), kind=kLoop, calls=%fused_computation.20 | loop fusion | flops 1703936 | bytes 2103296 | tf_op jit(solution)/shard_map/add | solution.py:218
  (30 shorter events, 0.3 us)
Async XLA Ops:
  0.0 10.9 %collective-permute-start = (bf16[1024,512]{1,0:T(8,128)(2,1)}, bf16[1024,512]{1,0:T(8,128)(2,1)S(1)}, u32[]{:S(2)}, u32[]{:S(2)}) collective-permute-start(bf16[1024,512]{1,0:T(8,128)(2,1)} %own_ref.5), channel_id=1, source_target_pairs={{0,4},{4,0},{1,5},{5,1},{2,6},{6,2},{3,7},{7,3},{8,12},{12,8},{9,1... | collective-permute-start | bytes 3145736 | tf_op jit(solution)/shard_map/ppermute | solution.py:119
  0.0 15.1 %collective-permute-start.1 = (bf16[1024,512]{1,0:T(8,128)(2,1)}, bf16[1024,512]{1,0:T(8,128)(2,1)S(1)}, u32[]{:S(2)}, u32[]{:S(2)}) collective-permute-start(bf16[1024,512]{1,0:T(8,128)(2,1)} %own_ref.5), channel_id=1, source_target_pairs={{4,8},{12,16},{20,24},{28,32},{36,40},{44,48},{52,56},{60,64},{68,... | collective-permute-start | bytes 3145736 | tf_op jit(solution)/shard_map/ppermute | solution.py:113
  0.7 24.5 %collective-permute-start.5 = (f32[1024,128]{1,0:T(8,128)}, f32[1024,128]{1,0:T(8,128)}, u32[]{:S(2)}, u32[]{:S(2)}) collective-permute-start(f32[1024,128]{1,0:T(8,128)} %param.5), channel_id=1, source_target_pairs={{0,4},{4,0},{1,5},{5,1},{2,6},{6,2},{3,7},{7,3},{8,12},{12,8},{9,1... | collective-permute-start | bytes 1572872 | tf_op jit(solution)/shard_map/ppermute | solution.py:119
  3.6 23.0 %collective-permute-start.3 = (f32[1024,128]{1,0:T(8,128)}, f32[1024,128]{1,0:T(8,128)S(1)}, u32[]{:S(2)}, u32[]{:S(2)}) collective-permute-start(f32[1024,128]{1,0:T(8,128)} %param.5), channel_id=1, source_target_pairs={{4,8},{12,16},{20,24},{28,32},{36,40},{44,48},{52,56},{60,64},{68,... | collective-permute-start | bytes 1572872 | tf_op jit(solution)/shard_map/ppermute | solution.py:113
  5.5 1.2 %copy-start = (bf16[1024,512]{1,0:T(8,128)(2,1)S(1)}, bf16[1024,512]{1,0:T(8,128)(2,1)}, u32[]{:S(2)}) copy-start(bf16[1024,512]{1,0:T(8,128)(2,1)} %own_ref.5) | copy-start | bytes 3145732
  10.9 12.2 %copy-start.1 = (f32[1024,128]{1,0:T(8,128)S(1)}, f32[1024,128]{1,0:T(8,128)}, u32[]{:S(2)}) copy-start(f32[1024,128]{1,0:T(8,128)} %param.5) | copy-start | bytes 1572868
  19.5 5.7 %collective-permute-start.4 = (f32[1024]{0:T(1024)S(1)}, f32[1024]{0:T(1024)S(1)}, u32[]{:S(2)}, u32[]{:S(2)}) collective-permute-start(f32[1024]{0:T(1024)S(1)} %rsqrt.7), channel_id=1, source_target_pairs={{0,4},{4,0},{1,5},{5,1},{2,6},{6,2},{3,7},{7,3},{8,12},{12,8},{9,1... | collective-permute-start | bytes 12296 | tf_op jit(solution)/shard_map/ppermute | solution.py:119
  22.5 4.1 %collective-permute-start.2 = (f32[1024]{0:T(1024)S(1)}, f32[1024]{0:T(1024)S(1)}, u32[]{:S(2)}, u32[]{:S(2)}) collective-permute-start(f32[1024]{0:T(1024)S(1)} %rsqrt.7), channel_id=1, source_target_pairs={{4,8},{12,16},{20,24},{28,32},{36,40},{44,48},{52,56},{60,64},{68,... | collective-permute-start | bytes 12296 | tf_op jit(solution)/shard_map/ppermute | solution.py:113
  30.8 8.4 %collective-permute-start.8 = (bf16[1024,256]{1,0:T(8,128)(2,1)S(1)}, bf16[1024,256]{1,0:T(8,128)(2,1)S(1)}, u32[]{:S(2)}, u32[]{:S(2)}) collective-permute-start(bf16[1024,256]{1,0:T(8,128)(2,1)S(1)} %pad_maximum_fusion.3.u_ref), channel_id=1, source_target_pairs={{0,4},{4,0},{1,5},{5,1},{2,6},{6,2},{3,7},{7,3},{8,12},{12,8},{9,1... | collective-permute-start | bytes 1572872 | tf_op jit(solution)/shard_map/ppermute | solution.py:119
  33.4 7.5 %collective-permute-start.7 = (bf16[1024,256]{1,0:T(8,128)(2,1)S(1)}, bf16[1024,256]{1,0:T(8,128)(2,1)S(1)}, u32[]{:S(2)}, u32[]{:S(2)}) collective-permute-start(bf16[1024,256]{1,0:T(8,128)(2,1)S(1)} %pad_maximum_fusion.3.u_ref), channel_id=1, source_target_pairs={{4,8},{12,16},{20,24},{28,32},{36,40},{44,48},{52,56},{60,64},{68,... | collective-permute-start | bytes 1572872 | tf_op jit(solution)/shard_map/ppermute | solution.py:113
  34.1 12.9 %collective-permute-start.6 = (f32[2,128]{1,0:T(2,128)S(1)}, f32[2,128]{1,0:T(2,128)S(1)}, u32[]{:S(2)}, u32[]{:S(2)}) collective-permute-start(f32[2,128]{1,0:T(2,128)S(1)} %pad_maximum_fusion.6), channel_id=1, source_target_pairs={{0,4},{4,0},{1,5},{5,1},{2,6},{6,2},{3,7},{7,3},{8,12},{12,8},{9,1... | collective-permute-start | bytes 3080 | tf_op jit(solution)/shard_map/ppermute | solution.py:119
  43.0 5.8 %collective-permute-start.10 = (bf16[1024,256]{1,0:T(8,128)(2,1)S(1)}, bf16[1024,256]{1,0:T(8,128)(2,1)S(1)}, u32[]{:S(2)}, u32[]{:S(2)}) collective-permute-start(bf16[1024,256]{1,0:T(8,128)(2,1)S(1)} %pad_maximum_fusion.4.u_ref), channel_id=1, source_target_pairs={{0,4},{4,0},{1,5},{5,1},{2,6},{6,2},{3,7},{7,3},{8,12},{12,8},{9,1... | collective-permute-start | bytes 1572872 | tf_op jit(solution)/shard_map/ppermute | solution.py:119
  46.3 4.3 %collective-permute-start.9 = (bf16[1024,256]{1,0:T(8,128)(2,1)S(1)}, bf16[1024,256]{1,0:T(8,128)(2,1)S(1)}, u32[]{:S(2)}, u32[]{:S(2)}) collective-permute-start(bf16[1024,256]{1,0:T(8,128)(2,1)S(1)} %pad_maximum_fusion.4.u_ref), channel_id=1, source_target_pairs={{4,8},{12,16},{20,24},{28,32},{36,40},{44,48},{52,56},{60,64},{68,... | collective-permute-start | bytes 1572872 | tf_op jit(solution)/shard_map/ppermute | solution.py:113
  53.0 7.7 %collective-permute-start.11 = (f32[9,128]{1,0:T(8,128)S(1)}, f32[9,128]{1,0:T(8,128)S(1)}, u32[]{:S(2)}, u32[]{:S(2)}) collective-permute-start(f32[9,128]{1,0:T(8,128)S(1)} %stack.64), channel_id=1, source_target_pairs={{0,4},{4,0},{1,5},{5,1},{2,6},{6,2},{3,7},{7,3},{8,12},{12,8},{9,1... | collective-permute-start | bytes 13832 | tf_op jit(solution)/shard_map/ppermute | solution.py:119

commit v2 on v1

v2 whole, which is shorter than its diff:
```python
import math

import jax
import jax.numpy as jnp
from jax import lax
from jax.experimental import pallas as pl
from jax.experimental.pallas import tpu as pltpu
from jax.sharding import Mesh, PartitionSpec as P


diffusion = 0.9
epsilon = 1e-06
tiny = 2e-07
smallest = 1e-37
f32 = jnp.float32
bf16 = jnp.bfloat16
ROWS = ("z", "x", "core")


def unit_rows(raw):
    values = raw.astype(f32)
    total = jnp.sum(values * values, axis=1, keepdims=True)
    return (values * lax.rsqrt(total + epsilon)).astype(bf16)


VECTOR = pl.BlockSpec(memory_space=pltpu.VMEM)
SCALAR = pl.BlockSpec(memory_space=pltpu.SMEM)


def kernel_call(kernel, scalars, arrays, outs, flops, moved, scratch=()):
    return pl.pallas_call(
        kernel,
        in_specs=[SCALAR] * len(scalars) + [VECTOR] * len(arrays),
        out_specs=[VECTOR] * len(outs),
        out_shape=[jax.ShapeDtypeStruct(*out) for out in outs],
        scratch_shapes=scratch,
        cost_estimate=pl.CostEstimate(flops=flops, bytes_accessed=moved, transcendentals=0),
        compiler_params=pltpu.CompilerParams(vmem_limit_bytes=16 << 20),
    )(*scalars, *arrays)


def affinity_kernel(neighbours, first, unit_ref, other_ref, w_ref, sums_ref, across_ref=None):
    blocks, slots = neighbours.shape
    rows = unit_ref.shape[0] // blocks
    half = rows // 2
    sums_ref[...] = jnp.zeros_like(sums_ref)
    for c in range(blocks):
        columns = pl.ds(c * rows, rows)
        other = other_ref[columns, :] if other_ref is unit_ref else unit_rows(other_ref[columns, :])
        across = None
        for b in range(blocks):
            linked = neighbours[b, 0] == first[0] + c
            for k in range(1, slots):
                linked = linked | (neighbours[b, k] == first[0] + c)
            similar = lax.dot_general(
                unit_ref[pl.ds(b * rows, rows), :],
                other,
                (((1,), (1,)), ((), ())),
                preferred_element_type=f32,
            )
            kept = jnp.maximum(similar, 0.0)
            w = kept * kept * (kept * jnp.where(linked, 1.0, 0.0).astype(f32))
            high = w.astype(bf16)
            w_ref[pl.ds(2 * b * rows, rows), columns] = high
            w_ref[pl.ds((2 * b + 1) * rows, rows), columns] = (w - high.astype(f32)).astype(bf16)
            sums_ref[pl.ds(b * rows, rows), :] += w[:, :half] + w[:, half:]
            if across_ref is not None:
                folded = jnp.sum(w.reshape(rows // 8, 8, rows), axis=0)
                across = folded if across is None else across + folded
        if across_ref is not None:
            across_ref[:, columns] = across


def own_affinity_kernel(neighbours, first, raw_ref, w_ref, sums_ref, unit_ref):
    unit_ref[...] = unit_rows(raw_ref[...])
    affinity_kernel(neighbours, first, unit_ref, unit_ref, w_ref, sums_ref)


def affinity(neighbours, block, own, other=None, both=False):
    n, features = own.shape
    outs = [((2 * n, n), bf16), ((n, 128), f32)]
    if other is None:
        outs.append(((n, features), bf16))
    if both:
        outs.append(((8, n), f32))
    return kernel_call(
        own_affinity_kernel if other is None else affinity_kernel,
        (neighbours, block.reshape(1)),
        (own,) if other is None else (own, other),
        outs,
        2 * n * n * features,
        8 * n * n,
    )


def product_kernel(w_ref, u_ref, base_ref, out_ref):
    n, columns = out_ref.shape
    rows = n // 4
    for b in range(4):
        part = pl.ds(b * rows, rows)
        wide = jnp.dot(w_ref[pl.ds(2 * b * rows, 2 * rows), :], u_ref[...], preferred_element_type=f32)
        both = wide[:rows] + wide[rows:]
        if u_ref.shape[1] > columns:
            both = both[:, :columns] + both[:, columns:]
        out_ref[part, :] = base_ref[part, :] + both


def first_product_kernel(w_ref, v_ref, scale_ref, base_ref, out_ref, u_ref):
    columns = v_ref.shape[1]
    values = v_ref[...] * scale_ref[...]
    high = values.astype(bf16)
    u_ref[:, :columns] = high
    u_ref[:, columns:] = (values - high.astype(f32)).astype(bf16)
    product_kernel(w_ref, u_ref, base_ref, out_ref)


def first_product(w, v, scale, base):
    n, columns = base.shape
    (out,) = kernel_call(
        first_product_kernel,
        (),
        (w, v, scale, base),
        [((n, columns), f32)],
        8 * n * n * columns,
        4 * n * n,
        scratch=[pltpu.VMEM((n, 2 * columns), bf16)],
    )
    return out


def product(w, split, base):
    n, columns = base.shape
    (out,) = kernel_call(
        product_kernel, (), (w, split, base), [((n, columns), f32)], 8 * n * n * columns, 4 * n * n
    )
    return out


def split(values):
    high = lax.reduce_precision(values, 8, 7)
    return jnp.concatenate([high.astype(bf16), (values - high).astype(bf16)], axis=1)


def outward(array):
    peers = math.prod(lax.axis_size(axis) for axis in ROWS)
    up = [(i, i + 1) for i in range(1, peers - 1, 2)]
    return lax.ppermute(array, ROWS, up + [(j, i) for i, j in up])


def swap(array):
    return lax.ppermute(array, "core", [(0, 1), (1, 0)])


def gathered(part):
    copies = jnp.broadcast_to(part[None], (32,) + part.shape).reshape(32, -1, 2, part.shape[1])
    return lax.all_to_all(copies, ("z", "x"), 0, 0).reshape((32,) + part.shape)


PAIRS = ((0, 0), (0, 1), (0, 2), (0, 3), (1, 1), (1, 2), (1, 3), (2, 2), (2, 3))
CHAIN = ((0, 0), (0, 1), (1, 1), (1, 2), (2, 2), (2, 3))


def moved(sums, d, pairs):
    powers = [jnp.ones_like(d)]
    for _ in range(5):
        powers.append(powers[-1] * d)
    out = {}
    for i, j in pairs:
        terms = [
            math.comb(i, a) * math.comb(j, c) * powers[i - a + j - c] * sums[min(a, c), max(a, c)]
            for a in range(i, -1, -1)
            for c in range(j, -1, -1)
        ]
        out[i, j] = sum(terms[1:], terms[0])
    return out


def unpacked(part):
    rows = [part[..., k, :] for k in range(len(PAIRS) + 1)]
    return dict(zip(PAIRS, rows)), rows[-1]


def both_cores(part):
    mine, my_shift = unpacked(part)
    theirs, their_shift = unpacked(swap(part))
    shift = 0.5 * (my_shift + their_shift)
    mine = moved(mine, my_shift - shift, PAIRS)
    theirs = moved(theirs, their_shift - shift, PAIRS)
    return jnp.stack([mine[p] + theirs[p] for p in PAIRS] + [shift])


def moments(parts):
    sums, own = unpacked(parts)
    mass = jnp.sum(sums[0, 0], axis=0)
    shift = jnp.sum(own * sums[0, 0] + sums[0, 1], axis=0) / mass
    central = moved(sums, own - shift[None], CHAIN)
    return shift, [jnp.sum(central[p], axis=0) for p in CHAIN]


def coefficients(shift, m):
    level = 1.0 - diffusion * shift
    h = [level * m[k] - diffusion * m[k + 1] for k in range(5)]
    least, most = 1.0 / (1.0 + diffusion), 1.0 / (1.0 - diffusion)
    l10 = h[1] / h[0]
    l20 = h[2] / h[0]
    d1 = jnp.maximum(h[2] - l10 * h[1], tiny * h[2])
    e21 = h[3] - l20 * h[1]
    l21 = e21 / d1
    d2 = jnp.maximum(h[4] - l20 * h[2] - l21 * e21, tiny * h[4])
    b0 = m[0]
    b1 = m[1] - l10 * b0
    b2 = m[2] - l20 * b0 - l21 * b1
    y0 = b0 / h[0]
    y1 = diffusion * y0 * jnp.clip(b1 / (d1 * diffusion * y0), least, most)
    y2 = diffusion * y1 * jnp.clip(b2 / (d2 * diffusion * y1), least, most)
    c2 = y2
    c1 = y1 - l21 * c2
    c0 = y0 - l10 * c1 - l20 * c2
    return c0, c1, c2


def powers(shift, g0, g1, g2):
    v1 = g1 - shift * g0
    t1 = g2 - shift * g1
    return v1, t1, t1 - shift * v1


def diffuse(embeddings, neighbours, queries):
    e_out, e_in = outward(embeddings), swap(embeddings)
    q_out, q_in = outward(queries), swap(queries)
    columns = queries.shape[1]
    blocks = neighbours.shape[0]
    index = lax.axis_index(ROWS)
    core = lax.axis_index("core")
    near, far = (index + 1 - 2 * core) * blocks, (index - 1 + 2 * core) * blocks
    w_own, deg_own, unit = affinity(neighbours, index * blocks, embeddings)
    w_in, deg_in = affinity(neighbours, near, unit, e_in)
    chip = jnp.sum(deg_own + deg_in, axis=1)
    unit, chip = lax.optimization_barrier((unit, chip))
    chip_out = outward(chip)
    w_out, deg_out, across = affinity(neighbours, far, unit, e_out, both=True)
    degree = chip + jnp.sum(jnp.maximum(deg_out, 0.0), axis=1)
    degree_in = swap(degree)
    degree_out = chip_out + jnp.sum(jnp.maximum(across, 0.0), axis=0)

    def wide_scale(sums):
        return lax.rsqrt(jnp.broadcast_to(jnp.maximum(sums, smallest)[:, None], queries.shape))

    column = wide_scale(degree)
    zero = jnp.zeros_like(queries)

    def apply(own, outer, inner):
        mixed = product(w_own, own, zero)
        mixed = product(w_in, inner, mixed)
        return column * product(w_out, outer, mixed)

    g0 = queries
    mixed = first_product(w_own, g0, column, zero)
    mixed = first_product(w_in, q_in, wide_scale(degree_in), mixed)
    g1 = column * first_product(w_out, q_out, wide_scale(degree_out), mixed)
    u1 = split(column * g1)
    g2 = apply(u1, outward(u1), swap(u1))
    u2 = split(column * g2)
    g3 = apply(u2, outward(u2[:, :columns]), swap(u2))
    mass, slope = jnp.sum(g0 * g0, axis=0), jnp.sum(g0 * g1, axis=0)
    own_shift = jnp.clip(jnp.where(mass > 0, slope / mass, 0.0), -1.0, 1.0)
    v1, t1, v2 = powers(own_shift, g0, g1, g2)
    v3 = (g3 - own_shift * g2) - own_shift * t1 - own_shift * v2
    v = (g0, v1, v2, v3)
    part = jnp.stack([jnp.sum(v[i] * v[j], axis=0) for i, j in PAIRS] + [own_shift])
    shift, m = moments(gathered(both_cores(part)))
    c0, c1, c2 = coefficients(shift, m)
    v1, _, v2 = powers(shift, g0, g1, g2)
    return c0 * g0 + c1 * v1 + c2 * v2


def solution(mesh):
    fine = Mesh(mesh.devices.reshape(8, 4, 2, 4), ("z", "x", "core", "cols"))
    placed = (P(ROWS, None), P(ROWS, None), P(ROWS, "cols"))
    return jax.shard_map(
        diffuse, mesh=fine, in_specs=placed, out_specs=P(ROWS, "cols"), check_vma=False
    )
```

time: 94.1 us -> 84.3 us (0.90)
  Pallas kernels: 28.5 us -> 19.5 us
  other arithmetic: 5.73 us -> 3.01 us
  local copies, waits for them, and re-layouts: 1.44 us -> 2.68 us
    pallas_call x12, Pallas kernels: 28.5 us -> 19.5 us  [kernel_call(): pl.pallas_call(kernel, in_specs=[SCALAR] * len(scalars) + [VECTOR] * len(...]
    convert_element_type x5 -> x1, other arithmetic: 1.86 us -> 0.2 us  [split(): (values - high).astype(bf16)]
    reduce_or x1 -> x0, other arithmetic: 1.03 us -> none  [shards(): jnp.any(neighbours[None, :, None, :] == candidates[:, None, :, None], axi...]
    ppermute x7 -> x6, starting transfers between devices: 21.9 us -> 22.6 us  [swap(): return lax.ppermute(array, 'core', [(0, 1), (1, 0)])]
    unnamed x4 -> x6, local copies, waits for them, and re-layouts: 1.23 us -> 1.91 us
  transfers between devices with their start and end apart: 12 -> 11, of which waited for: 1 -> 1; matrix products, arithmetic and copies ran while one was open for 4% -> 1% of each run, Pallas kernels for 25% -> 19%
where the time goes in v2:
time: 84.3 us; the launch traced here: 83.9 us
  blocking collectives  31.3 us (37%)
  starting transfers between devices  26.2 us (31%)
  Pallas kernels  19.5 us (23%)
  other arithmetic  3.01 us (4%)
  local copies, waits for them, and re-layouts  2.68 us (3%)
  waiting for transfers between devices  0.85 us (1%)
    all_to_all x1, blocking collectives, gathered(): return lax.all_to_all(copies, ('z', 'x'), 0, 0).reshape((32,) + part.shape)  31.3 us
    ppermute x6, starting transfers between devices, swap(): return lax.ppermute(array, 'core', [(0, 1), (1, 0)])  22.6 us
    pallas_call x12, Pallas kernels, kernel_call(): pl.pallas_call(kernel, in_specs=[SCALAR] * len(scalars) + [VECTOR] * len(...  19.5 us
    ppermute x5, starting transfers between devices, outward(): return lax.ppermute(array, ROWS, up + [(j, i) for i, j in up])  3.6 us
    unnamed x6, local copies, waits for them, and re-layouts  1.91 us
  transfers between devices with their start and end apart: 11, of which 1 were waited for; matrix products, arithmetic and copies ran while one was open for 1% of the time, Pallas kernels for 19%

profile of v2, /device:TPU:16, one launch (start us, length us, event | category | flops | bytes accessed | tf_op | source)
XLA Modules:
  0.0 83.9 jit_solution(4810258014171172072)
XLA Ops:
  0.0 0.0 collective-permute-start
  0.0 0.7 collective-permute-start.1
  0.7 2.9 %collective-permute-start.4 = (f32[1024,128]{1,0:T(8,128)}, f32[1024,128]{1,0:T(8,128)S(1)}, u32[]{:S(2)}, u32[]{:S(2)}) collective-permute-start(f32[1024,128]{1,0:T(8,128)} %v_ref.1), channel_id=1, source_target_pairs={{0,4},{4,0},{1,5},{5,1},{2,6},{6,2},{3,7},{7,3},{8,12},{12,8},{9,1... | collective-permute-start | bytes 1572872 | tf_op jit(solution)/shard_map/ppermute | solution.py:151
  3.6 0.7 collective-permute-start.2
  4.3 1.2 %copy-done.1 = bf16[1024,512]{1,0:T(8,128)(2,1)S(1)} copy-done((bf16[1024,512]{1,0:T(8,128)(2,1)S(1)}, bf16[1024,512]{1,0:T(8,128)(2,1)}, u32[]{:S(2)}) %copy-start.1) | copy-done | bytes 1048600
  5.5 0.7 copy-done.2
  6.2 2.2 %shard_map.37 = (bf16[2048,1024]{1,0:T(8,128)(2,1)S(1)}, f32[1024,128]{1,0:T(8,128)S(1)}, bf16[1024,512]{1,0:T(8,128)(2,1)S(1)}) custom-call(s32[4,12]{1,0:T(4,128)S(1)} %copy-done.2, s32[1]{0:T(128)} %bitcast.1.first, bf16[1024,512]{1,0:T(8,128)(2,1)S(1)} %copy-done.1), custom_call_target="tpu_custom_call" | custom-call | flops 1073741824 | bytes 8388608 | tf_op jit(solution)/shard_map/pallas_call | solution.py:31
  8.5 0.0 collective-permute-done.other_ref
  8.5 3.1 %shard_map.38 = (bf16[2048,1024]{1,0:T(8,128)(2,1)S(1)}, f32[1024,128]{1,0:T(8,128)S(1)}) custom-call(s32[4,12]{1,0:T(4,128)S(1)} %copy-done.2, s32[1]{0:T(128)} %bitcast.2.first, bf16[1024,512]{1,0:T(8,128)(2,1)S(1)} %get-tuple-element.19.unit_ref, bf16[1024,512]{1,0:T(8,128)(2,1)} %collective-permute-done.other_ref), custom_call_target="tpu_custom_call" | custom-call | flops 1073741824 | bytes 8388608 | tf_op jit(solution)/shard_map/pallas_call | solution.py:31
  11.6 0.0 copy-start
  11.6 0.2 add_reduce_fusion
  11.8 0.0 collective-permute-done.1.other_ref
  11.9 2.6 %shard_map.39 = (bf16[2048,1024]{1,0:T(8,128)(2,1)S(1)}, f32[1024,128]{1,0:T(8,128)S(1)}, f32[8,1024]{1,0:T(8,128)S(1)}) custom-call(s32[4,12]{1,0:T(4,128)S(1)} %copy-done.2, s32[1]{0:T(128)} %bitcast.3.first, bf16[1024,512]{1,0:T(8,128)(2,1)S(1)} %get-tuple-element.19.unit_ref, bf16[1024,512]{1,0:T(8,128)(2,1)S(1)} %collective-permute-done.1.other_ref), custom_call_target="tpu_custom_call" | custom-call | flops 1073741824 | bytes 8388608 | tf_op jit(solution)/shard_map/pallas_call | solution.py:31
  14.5 0.2 maximum_reduce_fusion
  14.7 0.7 collective-permute-start.3
  15.4 7.4 %collective-permute-start.5 = (f32[1024]{0:T(1024)S(1)}, f32[1024]{0:T(1024)S(1)}, u32[]{:S(2)}, u32[]{:S(2)}) collective-permute-start(f32[1024]{0:T(1024)S(1)} %get-tuple-element.57), channel_id=1, source_target_pairs={{0,4},{4,0},{1,5},{5,1},{2,6},{6,2},{3,7},{7,3},{8,12},{12,8},{9,1... | collective-permute-start | bytes 12296 | tf_op jit(solution)/shard_map/ppermute | solution.py:151
  22.8 0.2 broadcast_in_dim.11.scale_ref
  23.0 1.3 %shard_map.40.base_ref = f32[1024,128]{1,0:T(8,128)S(1)} custom-call(bf16[2048,1024]{1,0:T(8,128)(2,1)S(1)} %get-tuple-element.24.w_ref, f32[1024,128]{1,0:T(8,128)S(1)} %copy-done, f32[1024,128]{1,0:T(8,128)S(1)} %broadcast_in_dim.11.scale_ref, f32[1024,128]{1,0:T(8,128)S(1)} %broadcast_21_base_ref.2.base_ref), custom_call_target="tpu_custom_call" | custom-call | flops 1073741824 | bytes 4194304 | tf_op jit(solution)/shard_map/pallas_call | solution.py:31
  24.3 0.0 collective-permute-done.5
  24.4 0.0 collective-permute-done.4.v_ref
  24.4 0.2 broadcast_in_dim.14.scale_ref
  24.6 1.3 %shard_map.41.base_ref = f32[1024,128]{1,0:T(8,128)S(1)} custom-call(bf16[2048,1024]{1,0:T(8,128)(2,1)S(1)} %get-tuple-element.23.w_ref, f32[1024,128]{1,0:T(8,128)S(1)} %collective-permute-done.4.v_ref, f32[1024,128]{1,0:T(8,128)S(1)} %broadcast_in_dim.14.scale_ref, f32[1024,128]{1,0:T(8,128)S(1)} %shard_map.40.base_ref), custom_call_target="tpu_custom_call" | custom-call | flops 1073741824 | bytes 4194304 | tf_op jit(solution)/shard_map/pallas_call | solution.py:31
  25.9 0.0 collective-permute-done.3
  26.0 0.2 broadcast_in_dim.12.scale_ref
  26.2 1.3 %shard_map.42 = f32[1024,128]{1,0:T(8,128)S(1)} custom-call(bf16[2048,1024]{1,0:T(8,128)(2,1)S(1)} %get-tuple-element.21.w_ref, f32[1024,128]{1,0:T(8,128)S(1)} %collective-permute-done.2.v_ref, f32[1024,128]{1,0:T(8,128)S(1)} %broadcast_in_dim.12.scale_ref, f32[1024,128]{1,0:T(8,128)S(1)} %shard_map.41.base_ref), custom_call_target="tpu_custom_call" | custom-call | flops 1073741824 | bytes 4194304 | tf_op jit(solution)/shard_map/pallas_call | solution.py:31
  27.5 0.2 multiply_reduce_fusion.8
  27.7 0.1 pad_maximum_fusion.u_ref
  27.8 0.1 collective-permute-start.7
  27.9 0.9 %collective-permute-start.6 = (bf16[1024,256]{1,0:T(8,128)(2,1)S(1)}, bf16[1024,256]{1,0:T(8,128)(2,1)S(1)}, u32[]{:S(2)}, u32[]{:S(2)}) collective-permute-start(bf16[1024,256]{1,0:T(8,128)(2,1)S(1)} %pad_maximum_fusion.u_ref), channel_id=1, source_target_pairs={{4,8},{12,16},{20,24},{28,32},{36,40},{44,48},{52,56},{60,64},{68,... | collective-permute-start | bytes 1572872 | tf_op jit(solution)/shard_map/ppermute | solution.py:147
  28.8 1.3 %shard_map.43.base_ref = f32[1024,128]{1,0:T(8,128)S(1)} custom-call(bf16[2048,1024]{1,0:T(8,128)(2,1)S(1)} %get-tuple-element.24.w_ref, bf16[1024,256]{1,0:T(8,128)(2,1)S(1)} %pad_maximum_fusion.u_ref, f32[1024,128]{1,0:T(8,128)S(1)} %broadcast_21_base_ref.2.base_ref), custom_call_target="tpu_custom_call" | custom-call | flops 1073741824 | bytes 4194304 | tf_op jit(solution)/shard_map/pallas_call | solution.py:31
  30.1 1.3 %shard_map.44.base_ref = f32[1024,128]{1,0:T(8,128)S(1)} custom-call(bf16[2048,1024]{1,0:T(8,128)(2,1)S(1)} %get-tuple-element.23.w_ref, bf16[1024,256]{1,0:T(8,128)(2,1)S(1)} %collective-permute-done.7.u_ref, f32[1024,128]{1,0:T(8,128)S(1)} %shard_map.43.base_ref), custom_call_target="tpu_custom_call" | custom-call | flops 1073741824 | bytes 4194304 | tf_op jit(solution)/shard_map/pallas_call | solution.py:31
  31.3 0.0 collective-permute-done.6.u_ref
  31.3 1.3 %shard_map.45 = f32[1024,128]{1,0:T(8,128)S(1)} custom-call(bf16[2048,1024]{1,0:T(8,128)(2,1)S(1)} %get-tuple-element.21.w_ref, bf16[1024,256]{1,0:T(8,128)(2,1)S(1)} %collective-permute-done.6.u_ref, f32[1024,128]{1,0:T(8,128)S(1)} %shard_map.44.base_ref), custom_call_target="tpu_custom_call" | custom-call | flops 1073741824 | bytes 4194304 | tf_op jit(solution)/shard_map/pallas_call | solution.py:31
  32.6 0.2 fusion.1
  32.8 0.1 pad_maximum_fusion.1.u_ref
  32.9 7.7 %collective-permute-start.9 = (bf16[1024,256]{1,0:T(8,128)(2,1)S(1)}, bf16[1024,256]{1,0:T(8,128)(2,1)S(1)}, u32[]{:S(2)}, u32[]{:S(2)}) collective-permute-start(bf16[1024,256]{1,0:T(8,128)(2,1)S(1)} %pad_maximum_fusion.1.u_ref), channel_id=1, source_target_pairs={{0,4},{4,0},{1,5},{5,1},{2,6},{6,2},{3,7},{7,3},{8,12},{12,8},{9,1... | collective-permute-start | bytes 1572872 | tf_op jit(solution)/shard_map/ppermute | solution.py:151
  40.5 0.7 collective-permute-start.8
  41.2 1.3 %shard_map.46.base_ref = f32[1024,128]{1,0:T(8,128)S(1)} custom-call(bf16[2048,1024]{1,0:T(8,128)(2,1)S(1)} %get-tuple-element.24.w_ref, bf16[1024,256]{1,0:T(8,128)(2,1)S(1)} %pad_maximum_fusion.1.u_ref, f32[1024,128]{1,0:T(8,128)S(1)} %broadcast_21_base_ref.2.base_ref), custom_call_target="tpu_custom_call" | custom-call | flops 1073741824 | bytes 4194304 | tf_op jit(solution)/shard_map/pallas_call | solution.py:31
  42.5 1.3 %shard_map.47.base_ref = f32[1024,128]{1,0:T(8,128)S(1)} custom-call(bf16[2048,1024]{1,0:T(8,128)(2,1)S(1)} %get-tuple-element.23.w_ref, bf16[1024,256]{1,0:T(8,128)(2,1)S(1)} %collective-permute-done.9.u_ref, f32[1024,128]{1,0:T(8,128)S(1)} %shard_map.46.base_ref), custom_call_target="tpu_custom_call" | custom-call | flops 1073741824 | bytes 4194304 | tf_op jit(solution)/shard_map/pallas_call | solution.py:31
  43.7 0.0 collective-permute-done.8.u_ref
  43.8 1.3 %shard_map.48 = f32[1024,128]{1,0:T(8,128)S(1)} custom-call(bf16[2048,1024]{1,0:T(8,128)(2,1)S(1)} %get-tuple-element.21.w_ref, bf16[1024,128]{1,0:T(8,128)(2,1)S(1)} %collective-permute-done.8.u_ref, f32[1024,128]{1,0:T(8,128)S(1)} %shard_map.47.base_ref), custom_call_target="tpu_custom_call" | custom-call | flops 1073741824 | bytes 4194304 | tf_op jit(solution)/shard_map/pallas_call | solution.py:31
  45.1 0.3 multiply_subtract_fusion
  45.4 0.3 multiply_reduce_fusion
  45.7 4.6 %collective-permute-start.10 = (f32[10,128]{1,0:T(8,128)S(1)}, f32[10,128]{1,0:T(8,128)S(1)}, u32[]{:S(2)}, u32[]{:S(2)}) collective-permute-start(f32[10,128]{1,0:T(8,128)S(1)} %stack.50), channel_id=1, source_target_pairs={{0,4},{4,0},{1,5},{5,1},{2,6},{6,2},{3,7},{7,3},{8,12},{12,8},{9,1... | collective-permute-start | bytes 15368 | tf_op jit(solution)/shard_map/ppermute | solution.py:151
  50.3 0.8 collective-permute-done.10
  51.3 31.3 %all_to_all.5 = f32[32,5,2,128]{3,2,1,0:T(2,128)S(1)} all-to-all(f32[32,5,2,128]{3,2,1,0:T(2,128)S(1)} %broadcast_in_dim.16), channel_id=1, replica_groups=mesh['z'=8,'x'=4,'core'=2,'cols'=4] {'z','x'}, dimensions={0} | all-to-all | bytes 327680 | tf_op jit(solution)/shard_map/all_to_all | solution.py:156
  82.7 0.1 fusion.8
  82.8 1.1 %multiply_add_fusion = f32[1024,128]{1,0:T(8,128)} fusion(f32[1024,128]{1,0:T(8,128)S(1)} %copy-done, f32[1024,128]{1,0:T(8,128)S(1)} %shard_map.45, f32[1024,128]{1,0:T(8,128)S(1)} %shard_map.42, f32[128]{0:T(128)S(1)} %get-tuple-element.42, f32[128]{0:T(128)S(1)} %div.118, f32[128]{0:T(128)S(1)} %get-tuple-element.41, f32[128]{0:T(128)S(1)} %get-tuple-element.40, ...), kind=kLoop, calls=%fused_computation.8 | loop fusion | flops 1703936 | bytes 2103296 | tf_op jit(solution)/shard_map/add | solution.py:274
  (28 shorter events, 0.5 us)
Async XLA Ops:
  0.0 8.5 %collective-permute-start = (bf16[1024,512]{1,0:T(8,128)(2,1)}, bf16[1024,512]{1,0:T(8,128)(2,1)}, u32[]{:S(2)}, u32[]{:S(2)}) collective-permute-start(bf16[1024,512]{1,0:T(8,128)(2,1)} %raw_ref.1), channel_id=1, source_target_pairs={{0,4},{4,0},{1,5},{5,1},{2,6},{6,2},{3,7},{7,3},{8,12},{12,8},{9,1... | collective-permute-start | bytes 3145736 | tf_op jit(solution)/shard_map/ppermute | solution.py:151
  0.0 11.8 %collective-permute-start.1 = (bf16[1024,512]{1,0:T(8,128)(2,1)}, bf16[1024,512]{1,0:T(8,128)(2,1)S(1)}, u32[]{:S(2)}, u32[]{:S(2)}) collective-permute-start(bf16[1024,512]{1,0:T(8,128)(2,1)} %raw_ref.1), channel_id=1, source_target_pairs={{4,8},{12,16},{20,24},{28,32},{36,40},{44,48},{52,56},{60,64},{68,... | collective-permute-start | bytes 3145736 | tf_op jit(solution)/shard_map/ppermute | solution.py:147
  0.7 23.6 %collective-permute-start.4 = (f32[1024,128]{1,0:T(8,128)}, f32[1024,128]{1,0:T(8,128)S(1)}, u32[]{:S(2)}, u32[]{:S(2)}) collective-permute-start(f32[1024,128]{1,0:T(8,128)} %v_ref.1), channel_id=1, source_target_pairs={{0,4},{4,0},{1,5},{5,1},{2,6},{6,2},{3,7},{7,3},{8,12},{12,8},{9,1... | collective-permute-start | bytes 1572872 | tf_op jit(solution)/shard_map/ppermute | solution.py:151
  3.6 22.3 %collective-permute-start.2 = (f32[1024,128]{1,0:T(8,128)}, f32[1024,128]{1,0:T(8,128)S(1)}, u32[]{:S(2)}, u32[]{:S(2)}) collective-permute-start(f32[1024,128]{1,0:T(8,128)} %v_ref.1), channel_id=1, source_target_pairs={{4,8},{12,16},{20,24},{28,32},{36,40},{44,48},{52,56},{60,64},{68,... | collective-permute-start | bytes 1572872 | tf_op jit(solution)/shard_map/ppermute | solution.py:147
  4.3 1.2 %copy-start.1 = (bf16[1024,512]{1,0:T(8,128)(2,1)S(1)}, bf16[1024,512]{1,0:T(8,128)(2,1)}, u32[]{:S(2)}) copy-start(bf16[1024,512]{1,0:T(8,128)(2,1)} %raw_ref.1) | copy-start | bytes 3145732
  5.5 0.7 copy-start.2
  11.6 11.4 %copy-start = (f32[1024,128]{1,0:T(8,128)S(1)}, f32[1024,128]{1,0:T(8,128)}, u32[]{:S(2)}) copy-start(f32[1024,128]{1,0:T(8,128)} %v_ref.1) | copy-start | bytes 1572868
  14.7 11.3 %collective-permute-start.3 = (f32[1024]{0:T(1024)S(1)}, f32[1024]{0:T(1024)S(1)}, u32[]{:S(2)}, u32[]{:S(2)}) collective-permute-start(f32[1024]{0:T(1024)S(1)} %add_reduce_fusion), channel_id=1, source_target_pairs={{4,8},{12,16},{20,24},{28,32},{36,40},{44,48},{52,56},{60,64},{68,... | collective-permute-start | bytes 12296 | tf_op jit(solution)/shard_map/ppermute | solution.py:147
  15.4 9.0 %collective-permute-start.5 = (f32[1024]{0:T(1024)S(1)}, f32[1024]{0:T(1024)S(1)}, u32[]{:S(2)}, u32[]{:S(2)}) collective-permute-start(f32[1024]{0:T(1024)S(1)} %get-tuple-element.57), channel_id=1, source_target_pairs={{0,4},{4,0},{1,5},{5,1},{2,6},{6,2},{3,7},{7,3},{8,12},{12,8},{9,1... | collective-permute-start | bytes 12296 | tf_op jit(solution)/shard_map/ppermute | solution.py:151
  27.8 2.2 %collective-permute-start.7 = (bf16[1024,256]{1,0:T(8,128)(2,1)S(1)}, bf16[1024,256]{1,0:T(8,128)(2,1)S(1)}, u32[]{:S(2)}, u32[]{:S(2)}) collective-permute-start(bf16[1024,256]{1,0:T(8,128)(2,1)S(1)} %pad_maximum_fusion.u_ref), channel_id=1, source_target_pairs={{0,4},{4,0},{1,5},{5,1},{2,6},{6,2},{3,7},{7,3},{8,12},{12,8},{9,1... | collective-permute-start | bytes 1572872 | tf_op jit(solution)/shard_map/ppermute | solution.py:151
  27.9 3.4 %collective-permute-start.6 = (bf16[1024,256]{1,0:T(8,128)(2,1)S(1)}, bf16[1024,256]{1,0:T(8,128)(2,1)S(1)}, u32[]{:S(2)}, u32[]{:S(2)}) collective-permute-start(bf16[1024,256]{1,0:T(8,128)(2,1)S(1)} %pad_maximum_fusion.u_ref), channel_id=1, source_target_pairs={{4,8},{12,16},{20,24},{28,32},{36,40},{44,48},{52,56},{60,64},{68,... | collective-permute-start | bytes 1572872 | tf_op jit(solution)/shard_map/ppermute | solution.py:147
  32.9 9.6 %collective-permute-start.9 = (bf16[1024,256]{1,0:T(8,128)(2,1)S(1)}, bf16[1024,256]{1,0:T(8,128)(2,1)S(1)}, u32[]{:S(2)}, u32[]{:S(2)}) collective-permute-start(bf16[1024,256]{1,0:T(8,128)(2,1)S(1)} %pad_maximum_fusion.1.u_ref), channel_id=1, source_target_pairs={{0,4},{4,0},{1,5},{5,1},{2,6},{6,2},{3,7},{7,3},{8,12},{12,8},{9,1... | collective-permute-start | bytes 1572872 | tf_op jit(solution)/shard_map/ppermute | solution.py:151
  40.5 3.2 %collective-permute-start.8 = (bf16[1024,128]{1,0:T(8,128)(2,1)S(1)}, bf16[1024,128]{1,0:T(8,128)(2,1)S(1)}, u32[]{:S(2)}, u32[]{:S(2)}) collective-permute-start(bf16[1024,128]{1,0:T(8,128)(2,1)S(1)} %get-tuple-element.59), channel_id=1, source_target_pairs={{4,8},{12,16},{20,24},{28,32},{36,40},{44,48},{52,56},{60,64},{68,... | collective-permute-start | bytes 786440 | tf_op jit(solution)/shard_map/ppermute | solution.py:147
  45.7 5.4 %collective-permute-start.10 = (f32[10,128]{1,0:T(8,128)S(1)}, f32[10,128]{1,0:T(8,128)S(1)}, u32[]{:S(2)}, u32[]{:S(2)}) collective-permute-start(f32[10,128]{1,0:T(8,128)S(1)} %stack.50), channel_id=1, source_target_pairs={{0,4},{4,0},{1,5},{5,1},{2,6},{6,2},{3,7},{7,3},{8,12},{12,8},{9,1... | collective-permute-start | bytes 15368 | tf_op jit(solution)/shard_map/ppermute | solution.py:151

commit v3 on v2

--- a/solution.py
+++ b/solution.py
@@ -98,10 +98,14 @@
     rows = n // 4
     for b in range(4):
         part = pl.ds(b * rows, rows)
-        wide = jnp.dot(w_ref[pl.ds(2 * b * rows, 2 * rows), :], u_ref[...], preferred_element_type=f32)
-        both = wide[:rows] + wide[rows:]
         if u_ref.shape[1] > columns:
+            stacked = w_ref[pl.ds(2 * b * rows, 2 * rows), :]
+            wide = jnp.dot(stacked, u_ref[...], preferred_element_type=f32)
+            both = wide[:rows] + wide[rows:]
             both = both[:, :columns] + both[:, columns:]
+        else:
+            high = w_ref[pl.ds(2 * b * rows, rows), :]
+            both = jnp.dot(high, u_ref[...], preferred_element_type=f32)
         out_ref[part, :] = base_ref[part, :] + both
 
 
@@ -261,13 +265,18 @@
     u1 = split(column * g1)
     g2 = apply(u1, outward(u1), swap(u1))
     u2 = split(column * g2)
-    g3 = apply(u2, outward(u2[:, :columns]), swap(u2))
+    u2_out, u2_in = outward(u2[:, :columns]), swap(u2)
+    g1, g2, u2 = lax.optimization_barrier((g1, g2, u2))
     mass, slope = jnp.sum(g0 * g0, axis=0), jnp.sum(g0 * g1, axis=0)
     own_shift = jnp.clip(jnp.where(mass > 0, slope / mass, 0.0), -1.0, 1.0)
     v1, t1, v2 = powers(own_shift, g0, g1, g2)
-    v3 = (g3 - own_shift * g2) - own_shift * t1 - own_shift * v2
-    v = (g0, v1, v2, v3)
-    part = jnp.stack([jnp.sum(v[i] * v[j], axis=0) for i, j in PAIRS] + [own_shift])
+    v = (g0, v1, v2, own_shift * (g2 + t1 + v2))
+    sums = {(i, j): jnp.sum(v[i] * v[j], axis=0) for i, j in PAIRS if j < 3}
+    v, sums = lax.optimization_barrier((v, sums))
+    g3 = apply(u2, u2_out, u2_in)
+    v3 = g3 - v[3]
+    sums.update({(i, 3): jnp.sum(v[i] * v3, axis=0) for i in range(3)})
+    part = jnp.stack([sums[p] for p in PAIRS] + [own_shift])
     shift, m = moments(gathered(both_cores(part)))
     c0, c1, c2 = coefficients(shift, m)
     v1, _, v2 = powers(shift, g0, g1, g2)

time: 84.3 us -> 83 us (0.985)
  transfers between devices with their start and end apart: 11 -> 11, of which waited for: 1 -> 1; matrix products, arithmetic and copies ran while one was open for 1% -> 2% of each run, Pallas kernels for 19% -> 19%
where the time goes in v3:
time: 83 us; the launch traced here: 82.6 us
  blocking collectives  31.3 us (38%)
  starting transfers between devices  25.4 us (31%)
  Pallas kernels  18.9 us (23%)
  other arithmetic  3.05 us (4%)
  local copies, waits for them, and re-layouts  2.67 us (3%)
  waiting for transfers between devices  0.85 us (1%)
    all_to_all x1, blocking collectives, gathered(): return lax.all_to_all(copies, ('z', 'x'), 0, 0).reshape((32,) + part.shape)  31.3 us
    ppermute x6, starting transfers between devices, swap(): return lax.ppermute(array, 'core', [(0, 1), (1, 0)])  21.8 us
    pallas_call x12, Pallas kernels, kernel_call(): pl.pallas_call(kernel, in_specs=[SCALAR] * len(scalars) + [VECTOR] * len(...  18.9 us
    ppermute x5, starting transfers between devices, outward(): return lax.ppermute(array, ROWS, up + [(j, i) for i, j in up])  3.6 us
    unnamed x6, local copies, waits for them, and re-layouts  1.91 us
  transfers between devices with their start and end apart: 11, of which 1 were waited for; matrix products, arithmetic and copies ran while one was open for 2% of the time, Pallas kernels for 19%

profile of v3, /device:TPU:16, one launch (start us, length us, event | category | flops | bytes accessed | tf_op | source)
XLA Modules:
  0.0 82.6 jit_solution(10048258143257919027)
XLA Ops:
  0.0 0.0 collective-permute-start
  0.0 0.7 collective-permute-start.1
  0.7 2.9 %collective-permute-start.4 = (f32[1024,128]{1,0:T(8,128)}, f32[1024,128]{1,0:T(8,128)S(1)}, u32[]{:S(2)}, u32[]{:S(2)}) collective-permute-start(f32[1024,128]{1,0:T(8,128)} %v_ref.1), channel_id=1, source_target_pairs={{0,4},{4,0},{1,5},{5,1},{2,6},{6,2},{3,7},{7,3},{8,12},{12,8},{9,1... | collective-permute-start | bytes 1572872 | tf_op jit(solution)/shard_map/ppermute | solution.py:155
  3.6 0.7 collective-permute-start.2
  4.3 1.2 %copy-done.1 = bf16[1024,512]{1,0:T(8,128)(2,1)S(1)} copy-done((bf16[1024,512]{1,0:T(8,128)(2,1)S(1)}, bf16[1024,512]{1,0:T(8,128)(2,1)}, u32[]{:S(2)}) %copy-start.1) | copy-done | bytes 1048600
  5.5 0.7 copy-done.2
  6.2 2.2 %shard_map.37 = (bf16[2048,1024]{1,0:T(8,128)(2,1)S(1)}, f32[1024,128]{1,0:T(8,128)S(1)}, bf16[1024,512]{1,0:T(8,128)(2,1)S(1)}) custom-call(s32[4,12]{1,0:T(4,128)S(1)} %copy-done.2, s32[1]{0:T(128)} %bitcast.first, bf16[1024,512]{1,0:T(8,128)(2,1)S(1)} %copy-done.1), custom_call_target="tpu_custom_call" | custom-call | flops 1073741824 | bytes 8388608 | tf_op jit(solution)/shard_map/pallas_call | solution.py:31
  8.5 0.0 collective-permute-done.other_ref
  8.5 3.1 %shard_map.38 = (bf16[2048,1024]{1,0:T(8,128)(2,1)S(1)}, f32[1024,128]{1,0:T(8,128)S(1)}) custom-call(s32[4,12]{1,0:T(4,128)S(1)} %copy-done.2, s32[1]{0:T(128)} %bitcast.1.first, bf16[1024,512]{1,0:T(8,128)(2,1)S(1)} %get-tuple-element.32.unit_ref, bf16[1024,512]{1,0:T(8,128)(2,1)} %collective-permute-done.other_ref), custom_call_target="tpu_custom_call" | custom-call | flops 1073741824 | bytes 8388608 | tf_op jit(solution)/shard_map/pallas_call | solution.py:31
  11.6 0.0 copy-start
  11.6 0.2 add_reduce_fusion
  11.8 0.0 collective-permute-done.1.other_ref
  11.9 2.6 %shard_map.39 = (bf16[2048,1024]{1,0:T(8,128)(2,1)S(1)}, f32[1024,128]{1,0:T(8,128)S(1)}, f32[8,1024]{1,0:T(8,128)S(1)}) custom-call(s32[4,12]{1,0:T(4,128)S(1)} %copy-done.2, s32[1]{0:T(128)} %bitcast.2.first, bf16[1024,512]{1,0:T(8,128)(2,1)S(1)} %get-tuple-element.32.unit_ref, bf16[1024,512]{1,0:T(8,128)(2,1)S(1)} %collective-permute-done.1.other_ref), custom_call_target="tpu_custom_call" | custom-call | flops 1073741824 | bytes 8388608 | tf_op jit(solution)/shard_map/pallas_call | solution.py:31
  14.5 0.2 maximum_reduce_fusion
  14.7 0.7 collective-permute-start.3
  15.4 7.4 %collective-permute-start.5 = (f32[1024]{0:T(1024)S(1)}, f32[1024]{0:T(1024)S(1)}, u32[]{:S(2)}, u32[]{:S(2)}) collective-permute-start(f32[1024]{0:T(1024)S(1)} %get-tuple-element.81), channel_id=1, source_target_pairs={{0,4},{4,0},{1,5},{5,1},{2,6},{6,2},{3,7},{7,3},{8,12},{12,8},{9,1... | collective-permute-start | bytes 12296 | tf_op jit(solution)/shard_map/ppermute | solution.py:155
  22.8 0.2 broadcast_in_dim.11.scale_ref
  23.0 1.3 %shard_map.40.base_ref = f32[1024,128]{1,0:T(8,128)S(1)} custom-call(bf16[2048,1024]{1,0:T(8,128)(2,1)S(1)} %get-tuple-element.37.w_ref, f32[1024,128]{1,0:T(8,128)S(1)} %copy-done, f32[1024,128]{1,0:T(8,128)S(1)} %broadcast_in_dim.11.scale_ref, f32[1024,128]{1,0:T(8,128)S(1)} %broadcast_21_base_ref.2.base_ref), custom_call_target="tpu_custom_call" | custom-call | flops 1073741824 | bytes 4194304 | tf_op jit(solution)/shard_map/pallas_call | solution.py:31
  24.4 0.0 collective-permute-done.4.v_ref
  24.4 0.2 broadcast_in_dim.14.scale_ref
  24.6 1.3 %shard_map.41.base_ref = f32[1024,128]{1,0:T(8,128)S(1)} custom-call(bf16[2048,1024]{1,0:T(8,128)(2,1)S(1)} %get-tuple-element.36.w_ref, f32[1024,128]{1,0:T(8,128)S(1)} %collective-permute-done.4.v_ref, f32[1024,128]{1,0:T(8,128)S(1)} %broadcast_in_dim.14.scale_ref, f32[1024,128]{1,0:T(8,128)S(1)} %shard_map.40.base_ref), custom_call_target="tpu_custom_call" | custom-call | flops 1073741824 | bytes 4194304 | tf_op jit(solution)/shard_map/pallas_call | solution.py:31
  25.9 0.0 collective-permute-done.3
  26.0 0.2 broadcast_in_dim.12.scale_ref
  26.2 1.3 %shard_map.42 = f32[1024,128]{1,0:T(8,128)S(1)} custom-call(bf16[2048,1024]{1,0:T(8,128)(2,1)S(1)} %get-tuple-element.34.w_ref, f32[1024,128]{1,0:T(8,128)S(1)} %collective-permute-done.2.v_ref, f32[1024,128]{1,0:T(8,128)S(1)} %broadcast_in_dim.12.scale_ref, f32[1024,128]{1,0:T(8,128)S(1)} %shard_map.41.base_ref), custom_call_target="tpu_custom_call" | custom-call | flops 1073741824 | bytes 4194304 | tf_op jit(solution)/shard_map/pallas_call | solution.py:31
  27.5 0.2 reduce-precision_convert_fusion.1
  27.7 0.1 pad_maximum_fusion.u_ref
  27.8 0.1 collective-permute-start.7
  27.9 0.9 %collective-permute-start.6 = (bf16[1024,256]{1,0:T(8,128)(2,1)S(1)}, bf16[1024,256]{1,0:T(8,128)(2,1)S(1)}, u32[]{:S(2)}, u32[]{:S(2)}) collective-permute-start(bf16[1024,256]{1,0:T(8,128)(2,1)S(1)} %pad_maximum_fusion.u_ref), channel_id=1, source_target_pairs={{4,8},{12,16},{20,24},{28,32},{36,40},{44,48},{52,56},{60,64},{68,... | collective-permute-start | bytes 1572872 | tf_op jit(solution)/shard_map/ppermute | solution.py:151
  28.8 1.3 %shard_map.43.base_ref = f32[1024,128]{1,0:T(8,128)S(1)} custom-call(bf16[2048,1024]{1,0:T(8,128)(2,1)S(1)} %get-tuple-element.37.w_ref, bf16[1024,256]{1,0:T(8,128)(2,1)S(1)} %pad_maximum_fusion.u_ref, f32[1024,128]{1,0:T(8,128)S(1)} %broadcast_21_base_ref.2.base_ref), custom_call_target="tpu_custom_call" | custom-call | flops 1073741824 | bytes 4194304 | tf_op jit(solution)/shard_map/pallas_call | solution.py:31
  30.0 0.0 collective-permute-done.7.u_ref
  30.0 1.3 %shard_map.44.base_ref = f32[1024,128]{1,0:T(8,128)S(1)} custom-call(bf16[2048,1024]{1,0:T(8,128)(2,1)S(1)} %get-tuple-element.36.w_ref, bf16[1024,256]{1,0:T(8,128)(2,1)S(1)} %collective-permute-done.7.u_ref, f32[1024,128]{1,0:T(8,128)S(1)} %shard_map.43.base_ref), custom_call_target="tpu_custom_call" | custom-call | flops 1073741824 | bytes 4194304 | tf_op jit(solution)/shard_map/pallas_call | solution.py:31
  31.3 1.3 %shard_map.45 = f32[1024,128]{1,0:T(8,128)S(1)} custom-call(bf16[2048,1024]{1,0:T(8,128)(2,1)S(1)} %get-tuple-element.34.w_ref, bf16[1024,256]{1,0:T(8,128)(2,1)S(1)} %collective-permute-done.6.u_ref, f32[1024,128]{1,0:T(8,128)S(1)} %shard_map.44.base_ref), custom_call_target="tpu_custom_call" | custom-call | flops 1073741824 | bytes 4194304 | tf_op jit(solution)/shard_map/pallas_call | solution.py:31
  32.6 0.2 reduce-precision_convert_fusion
  32.8 0.7 collective-permute-start.8
  33.5 0.1 pad_maximum_fusion.1.u_ref
  33.5 10.0 %collective-permute-start.9 = (bf16[1024,256]{1,0:T(8,128)(2,1)S(1)}, bf16[1024,256]{1,0:T(8,128)(2,1)S(1)}, u32[]{:S(2)}, u32[]{:S(2)}) collective-permute-start(bf16[1024,256]{1,0:T(8,128)(2,1)S(1)} %pad_maximum_fusion.1.u_ref), channel_id=1, source_target_pairs={{0,4},{4,0},{1,5},{5,1},{2,6},{6,2},{3,7},{7,3},{8,12},{12,8},{9,1... | collective-permute-start | bytes 1572872 | tf_op jit(solution)/shard_map/ppermute | solution.py:155
  43.5 0.2 multiply_reduce_fusion.8
  43.7 0.3 multiply_reduce_fusion.3
  44.0 0.1 add_multiply_fusion
  44.1 1.3 %shard_map.46.base_ref = f32[1024,128]{1,0:T(8,128)S(1)} custom-call(bf16[2048,1024]{1,0:T(8,128)(2,1)S(1)} %get-tuple-element.37.w_ref, bf16[1024,256]{1,0:T(8,128)(2,1)S(1)} %pad_maximum_fusion.1.u_ref, f32[1024,128]{1,0:T(8,128)S(1)} %broadcast_21_base_ref.2.base_ref), custom_call_target="tpu_custom_call" | custom-call | flops 1073741824 | bytes 4194304 | tf_op jit(solution)/shard_map/pallas_call | solution.py:31
  45.4 1.3 %shard_map.47.base_ref = f32[1024,128]{1,0:T(8,128)S(1)} custom-call(bf16[2048,1024]{1,0:T(8,128)(2,1)S(1)} %get-tuple-element.36.w_ref, bf16[1024,256]{1,0:T(8,128)(2,1)S(1)} %collective-permute-done.9.u_ref, f32[1024,128]{1,0:T(8,128)S(1)} %shard_map.46.base_ref), custom_call_target="tpu_custom_call" | custom-call | flops 1073741824 | bytes 4194304 | tf_op jit(solution)/shard_map/pallas_call | solution.py:31
  46.7 0.7 shard_map.48
  47.4 0.2 multiply_reduce_fusion
  47.7 1.4 %collective-permute-start.10 = (f32[10,128]{1,0:T(8,128)S(1)}, f32[10,128]{1,0:T(8,128)S(1)}, u32[]{:S(2)}, u32[]{:S(2)}) collective-permute-start(f32[10,128]{1,0:T(8,128)S(1)} %stack.71), channel_id=1, source_target_pairs={{0,4},{4,0},{1,5},{5,1},{2,6},{6,2},{3,7},{7,3},{8,12},{12,8},{9,1... | collective-permute-start | bytes 15368 | tf_op jit(solution)/shard_map/ppermute | solution.py:155
  49.1 0.8 %collective-permute-done.10 = f32[10,128]{1,0:T(8,128)S(1)} collective-permute-done((f32[10,128]{1,0:T(8,128)S(1)}, f32[10,128]{1,0:T(8,128)S(1)}, u32[]{:S(2)}, u32[]{:S(2)}) %collective-permute-start.10) | collective-permute-done | bytes 5152 | tf_op jit(solution)/shard_map/ppermute | solution.py:155
  50.1 31.3 %all_to_all.5 = f32[32,5,2,128]{3,2,1,0:T(2,128)S(1)} all-to-all(f32[32,5,2,128]{3,2,1,0:T(2,128)S(1)} %broadcast_in_dim.16), channel_id=1, replica_groups=mesh['z'=8,'x'=4,'core'=2,'cols'=4] {'z','x'}, dimensions={0} | all-to-all | bytes 327680 | tf_op jit(solution)/shard_map/all_to_all | solution.py:160
  81.5 0.1 fusion.8
  81.6 1.0 %multiply_add_fusion = f32[1024,128]{1,0:T(8,128)} fusion(f32[1024,128]{1,0:T(8,128)S(1)} %get-tuple-element.39, f32[1024,128]{1,0:T(8,128)S(1)} %get-tuple-element.38, f32[1024,128]{1,0:T(8,128)S(1)} %copy-done, f32[128]{0:T(128)S(1)} %get-tuple-element.68, f32[128]{0:T(128)S(1)} %div.108, f32[128]{0:T(128)S(1)} %get-tuple-element.67, ...), kind=kLoop, calls=%fused_computation.8 | loop fusion | flops 1441792 | bytes 2099200 | tf_op jit(solution)/shard_map/add | solution.py:283
  (30 shorter events, 0.5 us)
Async XLA Ops:
  0.0 8.5 %collective-permute-start = (bf16[1024,512]{1,0:T(8,128)(2,1)}, bf16[1024,512]{1,0:T(8,128)(2,1)}, u32[]{:S(2)}, u32[]{:S(2)}) collective-permute-start(bf16[1024,512]{1,0:T(8,128)(2,1)} %raw_ref.1), channel_id=1, source_target_pairs={{0,4},{4,0},{1,5},{5,1},{2,6},{6,2},{3,7},{7,3},{8,12},{12,8},{9,1... | collective-permute-start | bytes 3145736 | tf_op jit(solution)/shard_map/ppermute | solution.py:155
  0.0 11.8 %collective-permute-start.1 = (bf16[1024,512]{1,0:T(8,128)(2,1)}, bf16[1024,512]{1,0:T(8,128)(2,1)S(1)}, u32[]{:S(2)}, u32[]{:S(2)}) collective-permute-start(bf16[1024,512]{1,0:T(8,128)(2,1)} %raw_ref.1), channel_id=1, source_target_pairs={{4,8},{12,16},{20,24},{28,32},{36,40},{44,48},{52,56},{60,64},{68,... | collective-permute-start | bytes 3145736 | tf_op jit(solution)/shard_map/ppermute | solution.py:151
  0.7 23.6 %collective-permute-start.4 = (f32[1024,128]{1,0:T(8,128)}, f32[1024,128]{1,0:T(8,128)S(1)}, u32[]{:S(2)}, u32[]{:S(2)}) collective-permute-start(f32[1024,128]{1,0:T(8,128)} %v_ref.1), channel_id=1, source_target_pairs={{0,4},{4,0},{1,5},{5,1},{2,6},{6,2},{3,7},{7,3},{8,12},{12,8},{9,1... | collective-permute-start | bytes 1572872 | tf_op jit(solution)/shard_map/ppermute | solution.py:155
  3.6 22.3 %collective-permute-start.2 = (f32[1024,128]{1,0:T(8,128)}, f32[1024,128]{1,0:T(8,128)S(1)}, u32[]{:S(2)}, u32[]{:S(2)}) collective-permute-start(f32[1024,128]{1,0:T(8,128)} %v_ref.1), channel_id=1, source_target_pairs={{4,8},{12,16},{20,24},{28,32},{36,40},{44,48},{52,56},{60,64},{68,... | collective-permute-start | bytes 1572872 | tf_op jit(solution)/shard_map/ppermute | solution.py:151
  4.3 1.2 %copy-start.1 = (bf16[1024,512]{1,0:T(8,128)(2,1)S(1)}, bf16[1024,512]{1,0:T(8,128)(2,1)}, u32[]{:S(2)}) copy-start(bf16[1024,512]{1,0:T(8,128)(2,1)} %raw_ref.1) | copy-start | bytes 3145732
  5.5 0.7 copy-start.2
  11.6 11.4 %copy-start = (f32[1024,128]{1,0:T(8,128)S(1)}, f32[1024,128]{1,0:T(8,128)}, u32[]{:S(2)}) copy-start(f32[1024,128]{1,0:T(8,128)} %v_ref.1) | copy-start | bytes 1572868
  14.7 11.3 %collective-permute-start.3 = (f32[1024]{0:T(1024)S(1)}, f32[1024]{0:T(1024)S(1)}, u32[]{:S(2)}, u32[]{:S(2)}) collective-permute-start(f32[1024]{0:T(1024)S(1)} %add_reduce_fusion), channel_id=1, source_target_pairs={{4,8},{12,16},{20,24},{28,32},{36,40},{44,48},{52,56},{60,64},{68,... | collective-permute-start | bytes 12296 | tf_op jit(solution)/shard_map/ppermute | solution.py:151
  15.4 9.0 %collective-permute-start.5 = (f32[1024]{0:T(1024)S(1)}, f32[1024]{0:T(1024)S(1)}, u32[]{:S(2)}, u32[]{:S(2)}) collective-permute-start(f32[1024]{0:T(1024)S(1)} %get-tuple-element.81), channel_id=1, source_target_pairs={{0,4},{4,0},{1,5},{5,1},{2,6},{6,2},{3,7},{7,3},{8,12},{12,8},{9,1... | collective-permute-start | bytes 12296 | tf_op jit(solution)/shard_map/ppermute | solution.py:155
  27.8 2.2 %collective-permute-start.7 = (bf16[1024,256]{1,0:T(8,128)(2,1)S(1)}, bf16[1024,256]{1,0:T(8,128)(2,1)S(1)}, u32[]{:S(2)}, u32[]{:S(2)}) collective-permute-start(bf16[1024,256]{1,0:T(8,128)(2,1)S(1)} %pad_maximum_fusion.u_ref), channel_id=1, source_target_pairs={{0,4},{4,0},{1,5},{5,1},{2,6},{6,2},{3,7},{7,3},{8,12},{12,8},{9,1... | collective-permute-start | bytes 1572872 | tf_op jit(solution)/shard_map/ppermute | solution.py:155
  27.9 3.4 %collective-permute-start.6 = (bf16[1024,256]{1,0:T(8,128)(2,1)S(1)}, bf16[1024,256]{1,0:T(8,128)(2,1)S(1)}, u32[]{:S(2)}, u32[]{:S(2)}) collective-permute-start(bf16[1024,256]{1,0:T(8,128)(2,1)S(1)} %pad_maximum_fusion.u_ref), channel_id=1, source_target_pairs={{4,8},{12,16},{20,24},{28,32},{36,40},{44,48},{52,56},{60,64},{68,... | collective-permute-start | bytes 1572872 | tf_op jit(solution)/shard_map/ppermute | solution.py:151
  32.8 13.9 %collective-permute-start.8 = (bf16[1024,128]{1,0:T(8,128)(2,1)S(1)}, bf16[1024,128]{1,0:T(8,128)(2,1)S(1)}, u32[]{:S(2)}, u32[]{:S(2)}) collective-permute-start(bf16[1024,128]{1,0:T(8,128)(2,1)S(1)} %get-tuple-element.82), channel_id=1, source_target_pairs={{4,8},{12,16},{20,24},{28,32},{36,40},{44,48},{52,56},{60,64},{68,... | collective-permute-start | bytes 786440 | tf_op jit(solution)/shard_map/ppermute | solution.py:151
  33.5 11.9 %collective-permute-start.9 = (bf16[1024,256]{1,0:T(8,128)(2,1)S(1)}, bf16[1024,256]{1,0:T(8,128)(2,1)S(1)}, u32[]{:S(2)}, u32[]{:S(2)}) collective-permute-start(bf16[1024,256]{1,0:T(8,128)(2,1)S(1)} %pad_maximum_fusion.1.u_ref), channel_id=1, source_target_pairs={{0,4},{4,0},{1,5},{5,1},{2,6},{6,2},{3,7},{7,3},{8,12},{12,8},{9,1... | collective-permute-start | bytes 1572872 | tf_op jit(solution)/shard_map/ppermute | solution.py:155
  47.7 2.2 %collective-permute-start.10 = (f32[10,128]{1,0:T(8,128)S(1)}, f32[10,128]{1,0:T(8,128)S(1)}, u32[]{:S(2)}, u32[]{:S(2)}) collective-permute-start(f32[10,128]{1,0:T(8,128)S(1)} %stack.71), channel_id=1, source_target_pairs={{0,4},{4,0},{1,5},{5,1},{2,6},{6,2},{3,7},{7,3},{8,12},{12,8},{9,1... | collective-permute-start | bytes 15368 | tf_op jit(solution)/shard_map/ppermute | solution.py:155

commit v4 on v3

--- a/solution.py
+++ b/solution.py
@@ -106,7 +106,11 @@
         else:
             high = w_ref[pl.ds(2 * b * rows, rows), :]
             both = jnp.dot(high, u_ref[...], preferred_element_type=f32)
-        out_ref[part, :] = base_ref[part, :] + both
+        out_ref[part, :] = both if base_ref is None else base_ref[part, :] + both
+
+
+def bare_product_kernel(w_ref, u_ref, out_ref):
+    product_kernel(w_ref, u_ref, None, out_ref)
 
 
 def first_product_kernel(w_ref, v_ref, scale_ref, base_ref, out_ref, u_ref):
@@ -118,12 +122,16 @@
     product_kernel(w_ref, u_ref, base_ref, out_ref)
 
 
-def first_product(w, v, scale, base):
-    n, columns = base.shape
+def bare_first_product_kernel(w_ref, v_ref, scale_ref, out_ref, u_ref):
+    first_product_kernel(w_ref, v_ref, scale_ref, None, out_ref, u_ref)
+
+
+def first_product(w, v, scale, *base):
+    n, columns = v.shape
     (out,) = kernel_call(
-        first_product_kernel,
+        first_product_kernel if base else bare_first_product_kernel,
         (),
-        (w, v, scale, base),
+        (w, v, scale) + base,
         [((n, columns), f32)],
         8 * n * n * columns,
         4 * n * n,
@@ -132,10 +140,15 @@
     return out
 
 
-def product(w, split, base):
-    n, columns = base.shape
+def product(w, split, columns, *base):
+    n = w.shape[1]
     (out,) = kernel_call(
-        product_kernel, (), (w, split, base), [((n, columns), f32)], 8 * n * n * columns, 4 * n * n
+        product_kernel if base else bare_product_kernel,
+        (),
+        (w, split) + base,
+        [((n, columns), f32)],
+        8 * n * n * columns,
+        4 * n * n,
     )
     return out
 
@@ -251,15 +264,14 @@
         return lax.rsqrt(jnp.broadcast_to(jnp.maximum(sums, smallest)[:, None], queries.shape))
 
     column = wide_scale(degree)
-    zero = jnp.zeros_like(queries)
 
     def apply(own, outer, inner):
-        mixed = product(w_own, own, zero)
-        mixed = product(w_in, inner, mixed)
-        return column * product(w_out, outer, mixed)
+        mixed = product(w_own, own, columns)
+        mixed = product(w_in, inner, columns, mixed)
+        return column * product(w_out, outer, columns, mixed)
 
     g0 = queries
-    mixed = first_product(w_own, g0, column, zero)
+    mixed = first_product(w_own, g0, column)
     mixed = first_product(w_in, q_in, wide_scale(degree_in), mixed)
     g1 = column * first_product(w_out, q_out, wide_scale(degree_out), mixed)
     u1 = split(column * g1)

time: 83 us -> 82.9 us (level)
  no operation moved by 1% of the time
where the time goes in v4:
time: 82.9 us; the launch traced here: 82.6 us
  blocking collectives  31.3 us (38%)
  starting transfers between devices  25.4 us (31%)
  Pallas kernels  19 us (23%)
  other arithmetic  3.05 us (4%)
  local copies, waits for them, and re-layouts  2.64 us (3%)
  waiting for transfers between devices  0.85 us (1%)
    all_to_all x1, blocking collectives, gathered(): return lax.all_to_all(copies, ('z', 'x'), 0, 0).reshape((32,) + part.shape)  31.3 us
    ppermute x6, starting transfers between devices, swap(): return lax.ppermute(array, 'core', [(0, 1), (1, 0)])  21.8 us
    pallas_call x12, Pallas kernels, kernel_call(): pl.pallas_call(kernel, in_specs=[SCALAR] * len(scalars) + [VECTOR] * len(...  19 us
    ppermute x5, starting transfers between devices, outward(): return lax.ppermute(array, ROWS, up + [(j, i) for i, j in up])  3.6 us
    unnamed x6, local copies, waits for them, and re-layouts  1.91 us
  transfers between devices with their start and end apart: 11, of which 1 were waited for; matrix products, arithmetic and copies ran while one was open for 2% of the time, Pallas kernels for 19%

profile of v4, /device:TPU:16, one launch (start us, length us, event | category | flops | bytes accessed | tf_op | source)
XLA Modules:
  0.0 82.6 jit_solution(4057238075397183230)
XLA Ops:
  0.0 0.0 collective-permute-start
  0.0 0.7 collective-permute-start.1
  0.7 2.9 %collective-permute-start.4 = (f32[1024,128]{1,0:T(8,128)}, f32[1024,128]{1,0:T(8,128)S(1)}, u32[]{:S(2)}, u32[]{:S(2)}) collective-permute-start(f32[1024,128]{1,0:T(8,128)} %v_ref.1), channel_id=1, source_target_pairs={{0,4},{4,0},{1,5},{5,1},{2,6},{6,2},{3,7},{7,3},{8,12},{12,8},{9,1... | collective-permute-start | bytes 1572872 | tf_op jit(solution)/shard_map/ppermute | solution.py:168
  3.6 0.7 collective-permute-start.2
  4.3 1.2 %copy-done.1 = bf16[1024,512]{1,0:T(8,128)(2,1)S(1)} copy-done((bf16[1024,512]{1,0:T(8,128)(2,1)S(1)}, bf16[1024,512]{1,0:T(8,128)(2,1)}, u32[]{:S(2)}) %copy-start.1) | copy-done | bytes 1048600
  5.5 0.7 copy-done.2
  6.2 2.2 %shard_map.37 = (bf16[2048,1024]{1,0:T(8,128)(2,1)S(1)}, f32[1024,128]{1,0:T(8,128)S(1)}, bf16[1024,512]{1,0:T(8,128)(2,1)S(1)}) custom-call(s32[4,12]{1,0:T(4,128)S(1)} %copy-done.2, s32[1]{0:T(128)} %bitcast.first, bf16[1024,512]{1,0:T(8,128)(2,1)S(1)} %copy-done.1), custom_call_target="tpu_custom_call" | custom-call | flops 1073741824 | bytes 8388608 | tf_op jit(solution)/shard_map/pallas_call | solution.py:31
  8.5 0.0 collective-permute-done.other_ref
  8.5 0.0 copy-start
  8.5 3.2 %shard_map.38 = (bf16[2048,1024]{1,0:T(8,128)(2,1)S(1)}, f32[1024,128]{1,0:T(8,128)S(1)}) custom-call(s32[4,12]{1,0:T(4,128)S(1)} %copy-done.2, s32[1]{0:T(128)} %bitcast.1.first, bf16[1024,512]{1,0:T(8,128)(2,1)S(1)} %get-tuple-element.32.unit_ref, bf16[1024,512]{1,0:T(8,128)(2,1)} %collective-permute-done.other_ref), custom_call_target="tpu_custom_call" | custom-call | flops 1073741824 | bytes 8388608 | tf_op jit(solution)/shard_map/pallas_call | solution.py:31
  11.7 0.2 add_reduce_fusion
  11.9 2.6 %shard_map.39 = (bf16[2048,1024]{1,0:T(8,128)(2,1)S(1)}, f32[1024,128]{1,0:T(8,128)S(1)}, f32[8,1024]{1,0:T(8,128)S(1)}) custom-call(s32[4,12]{1,0:T(4,128)S(1)} %copy-done.2, s32[1]{0:T(128)} %bitcast.2.first, bf16[1024,512]{1,0:T(8,128)(2,1)S(1)} %get-tuple-element.32.unit_ref, bf16[1024,512]{1,0:T(8,128)(2,1)S(1)} %collective-permute-done.1.other_ref), custom_call_target="tpu_custom_call" | custom-call | flops 1073741824 | bytes 8388608 | tf_op jit(solution)/shard_map/pallas_call | solution.py:31
  14.5 0.2 maximum_reduce_fusion
  14.7 0.7 collective-permute-start.3
  15.4 7.3 %collective-permute-start.5 = (f32[1024]{0:T(1024)S(1)}, f32[1024]{0:T(1024)S(1)}, u32[]{:S(2)}, u32[]{:S(2)}) collective-permute-start(f32[1024]{0:T(1024)S(1)} %get-tuple-element.81), channel_id=1, source_target_pairs={{0,4},{4,0},{1,5},{5,1},{2,6},{6,2},{3,7},{7,3},{8,12},{12,8},{9,1... | collective-permute-start | bytes 12296 | tf_op jit(solution)/shard_map/ppermute | solution.py:168
  22.8 0.2 broadcast_in_dim.11.scale_ref
  23.0 1.3 %shard_map.40.base_ref = f32[1024,128]{1,0:T(8,128)S(1)} custom-call(bf16[2048,1024]{1,0:T(8,128)(2,1)S(1)} %get-tuple-element.37.w_ref, f32[1024,128]{1,0:T(8,128)S(1)} %copy-done, f32[1024,128]{1,0:T(8,128)S(1)} %broadcast_in_dim.11.scale_ref), custom_call_target="tpu_custom_call" | custom-call | flops 1073741824 | bytes 4194304 | tf_op jit(solution)/shard_map/pallas_call | solution.py:31
  24.3 0.0 collective-permute-done.5
  24.3 0.2 broadcast_in_dim.14.scale_ref
  24.5 1.3 %shard_map.41.base_ref = f32[1024,128]{1,0:T(8,128)S(1)} custom-call(bf16[2048,1024]{1,0:T(8,128)(2,1)S(1)} %get-tuple-element.36.w_ref, f32[1024,128]{1,0:T(8,128)S(1)} %collective-permute-done.4.v_ref, f32[1024,128]{1,0:T(8,128)S(1)} %broadcast_in_dim.14.scale_ref, f32[1024,128]{1,0:T(8,128)S(1)} %shard_map.40.base_ref), custom_call_target="tpu_custom_call" | custom-call | flops 1073741824 | bytes 4194304 | tf_op jit(solution)/shard_map/pallas_call | solution.py:31
  25.9 0.0 collective-permute-done.3
  25.9 0.2 broadcast_in_dim.12.scale_ref
  26.1 1.3 %shard_map.42 = f32[1024,128]{1,0:T(8,128)S(1)} custom-call(bf16[2048,1024]{1,0:T(8,128)(2,1)S(1)} %get-tuple-element.34.w_ref, f32[1024,128]{1,0:T(8,128)S(1)} %collective-permute-done.2.v_ref, f32[1024,128]{1,0:T(8,128)S(1)} %broadcast_in_dim.12.scale_ref, f32[1024,128]{1,0:T(8,128)S(1)} %shard_map.41.base_ref), custom_call_target="tpu_custom_call" | custom-call | flops 1073741824 | bytes 4194304 | tf_op jit(solution)/shard_map/pallas_call | solution.py:31
  27.4 0.2 reduce-precision_convert_fusion.1
  27.7 0.1 pad_maximum_fusion.u_ref
  27.7 0.1 collective-permute-start.7
  27.8 0.9 %collective-permute-start.6 = (bf16[1024,256]{1,0:T(8,128)(2,1)S(1)}, bf16[1024,256]{1,0:T(8,128)(2,1)S(1)}, u32[]{:S(2)}, u32[]{:S(2)}) collective-permute-start(bf16[1024,256]{1,0:T(8,128)(2,1)S(1)} %pad_maximum_fusion.u_ref), channel_id=1, source_target_pairs={{4,8},{12,16},{20,24},{28,32},{36,40},{44,48},{52,56},{60,64},{68,... | collective-permute-start | bytes 1572872 | tf_op jit(solution)/shard_map/ppermute | solution.py:164
  28.7 1.2 %shard_map.43.base_ref = f32[1024,128]{1,0:T(8,128)S(1)} custom-call(bf16[2048,1024]{1,0:T(8,128)(2,1)S(1)} %get-tuple-element.37.w_ref, bf16[1024,256]{1,0:T(8,128)(2,1)S(1)} %pad_maximum_fusion.u_ref), custom_call_target="tpu_custom_call" | custom-call | flops 1073741824 | bytes 4194304 | tf_op jit(solution)/shard_map/pallas_call | solution.py:31
  30.0 0.0 collective-permute-done.7.u_ref
  30.0 1.3 %shard_map.44.base_ref = f32[1024,128]{1,0:T(8,128)S(1)} custom-call(bf16[2048,1024]{1,0:T(8,128)(2,1)S(1)} %get-tuple-element.36.w_ref, bf16[1024,256]{1,0:T(8,128)(2,1)S(1)} %collective-permute-done.7.u_ref, f32[1024,128]{1,0:T(8,128)S(1)} %shard_map.43.base_ref), custom_call_target="tpu_custom_call" | custom-call | flops 1073741824 | bytes 4194304 | tf_op jit(solution)/shard_map/pallas_call | solution.py:31
  31.2 0.0 collective-permute-done.6.u_ref
  31.2 1.3 %shard_map.45 = f32[1024,128]{1,0:T(8,128)S(1)} custom-call(bf16[2048,1024]{1,0:T(8,128)(2,1)S(1)} %get-tuple-element.34.w_ref, bf16[1024,256]{1,0:T(8,128)(2,1)S(1)} %collective-permute-done.6.u_ref, f32[1024,128]{1,0:T(8,128)S(1)} %shard_map.44.base_ref), custom_call_target="tpu_custom_call" | custom-call | flops 1073741824 | bytes 4194304 | tf_op jit(solution)/shard_map/pallas_call | solution.py:31
  32.5 0.2 reduce-precision_convert_fusion
  32.7 0.7 collective-permute-start.8
  33.4 0.1 pad_maximum_fusion.1.u_ref
  33.5 10.0 %collective-permute-start.9 = (bf16[1024,256]{1,0:T(8,128)(2,1)S(1)}, bf16[1024,256]{1,0:T(8,128)(2,1)S(1)}, u32[]{:S(2)}, u32[]{:S(2)}) collective-permute-start(bf16[1024,256]{1,0:T(8,128)(2,1)S(1)} %pad_maximum_fusion.1.u_ref), channel_id=1, source_target_pairs={{0,4},{4,0},{1,5},{5,1},{2,6},{6,2},{3,7},{7,3},{8,12},{12,8},{9,1... | collective-permute-start | bytes 1572872 | tf_op jit(solution)/shard_map/ppermute | solution.py:168
  43.5 0.2 multiply_reduce_fusion.8
  43.7 0.3 multiply_reduce_fusion.3
  44.0 0.1 add_multiply_fusion
  44.1 1.3 %shard_map.46.base_ref = f32[1024,128]{1,0:T(8,128)S(1)} custom-call(bf16[2048,1024]{1,0:T(8,128)(2,1)S(1)} %get-tuple-element.37.w_ref, bf16[1024,256]{1,0:T(8,128)(2,1)S(1)} %pad_maximum_fusion.1.u_ref), custom_call_target="tpu_custom_call" | custom-call | flops 1073741824 | bytes 4194304 | tf_op jit(solution)/shard_map/pallas_call | solution.py:31
  45.4 1.3 %shard_map.47.base_ref = f32[1024,128]{1,0:T(8,128)S(1)} custom-call(bf16[2048,1024]{1,0:T(8,128)(2,1)S(1)} %get-tuple-element.36.w_ref, bf16[1024,256]{1,0:T(8,128)(2,1)S(1)} %collective-permute-done.9.u_ref, f32[1024,128]{1,0:T(8,128)S(1)} %shard_map.46.base_ref), custom_call_target="tpu_custom_call" | custom-call | flops 1073741824 | bytes 4194304 | tf_op jit(solution)/shard_map/pallas_call | solution.py:31
  46.6 0.7 shard_map.48
  47.3 0.2 multiply_reduce_fusion
  47.6 1.4 %collective-permute-start.10 = (f32[10,128]{1,0:T(8,128)S(1)}, f32[10,128]{1,0:T(8,128)S(1)}, u32[]{:S(2)}, u32[]{:S(2)}) collective-permute-start(f32[10,128]{1,0:T(8,128)S(1)} %stack.71), channel_id=1, source_target_pairs={{0,4},{4,0},{1,5},{5,1},{2,6},{6,2},{3,7},{7,3},{8,12},{12,8},{9,1... | collective-permute-start | bytes 15368 | tf_op jit(solution)/shard_map/ppermute | solution.py:168
  49.0 0.8 %collective-permute-done.10 = f32[10,128]{1,0:T(8,128)S(1)} collective-permute-done((f32[10,128]{1,0:T(8,128)S(1)}, f32[10,128]{1,0:T(8,128)S(1)}, u32[]{:S(2)}, u32[]{:S(2)}) %collective-permute-start.10) | collective-permute-done | bytes 5152 | tf_op jit(solution)/shard_map/ppermute | solution.py:168
  50.1 31.3 %all_to_all.5 = f32[32,5,2,128]{3,2,1,0:T(2,128)S(1)} all-to-all(f32[32,5,2,128]{3,2,1,0:T(2,128)S(1)} %broadcast_in_dim.16), channel_id=1, replica_groups=mesh['z'=8,'x'=4,'core'=2,'cols'=4] {'z','x'}, dimensions={0} | all-to-all | bytes 327680 | tf_op jit(solution)/shard_map/all_to_all | solution.py:173
  81.5 0.1 fusion.8
  81.6 1.0 %multiply_add_fusion = f32[1024,128]{1,0:T(8,128)} fusion(f32[1024,128]{1,0:T(8,128)S(1)} %get-tuple-element.39, f32[1024,128]{1,0:T(8,128)S(1)} %get-tuple-element.38, f32[1024,128]{1,0:T(8,128)S(1)} %copy-done, f32[128]{0:T(128)S(1)} %get-tuple-element.68, f32[128]{0:T(128)S(1)} %div.108, f32[128]{0:T(128)S(1)} %get-tuple-element.67, ...), kind=kLoop, calls=%fused_computation.8 | loop fusion | flops 1441792 | bytes 2099200 | tf_op jit(solution)/shard_map/add | solution.py:295
  (29 shorter events, 0.4 us)
Async XLA Ops:
  0.0 8.5 %collective-permute-start = (bf16[1024,512]{1,0:T(8,128)(2,1)}, bf16[1024,512]{1,0:T(8,128)(2,1)}, u32[]{:S(2)}, u32[]{:S(2)}) collective-permute-start(bf16[1024,512]{1,0:T(8,128)(2,1)} %raw_ref.1), channel_id=1, source_target_pairs={{0,4},{4,0},{1,5},{5,1},{2,6},{6,2},{3,7},{7,3},{8,12},{12,8},{9,1... | collective-permute-start | bytes 3145736 | tf_op jit(solution)/shard_map/ppermute | solution.py:168
  0.0 11.9 %collective-permute-start.1 = (bf16[1024,512]{1,0:T(8,128)(2,1)}, bf16[1024,512]{1,0:T(8,128)(2,1)S(1)}, u32[]{:S(2)}, u32[]{:S(2)}) collective-permute-start(bf16[1024,512]{1,0:T(8,128)(2,1)} %raw_ref.1), channel_id=1, source_target_pairs={{4,8},{12,16},{20,24},{28,32},{36,40},{44,48},{52,56},{60,64},{68,... | collective-permute-start | bytes 3145736 | tf_op jit(solution)/shard_map/ppermute | solution.py:164
  0.7 23.6 %collective-permute-start.4 = (f32[1024,128]{1,0:T(8,128)}, f32[1024,128]{1,0:T(8,128)S(1)}, u32[]{:S(2)}, u32[]{:S(2)}) collective-permute-start(f32[1024,128]{1,0:T(8,128)} %v_ref.1), channel_id=1, source_target_pairs={{0,4},{4,0},{1,5},{5,1},{2,6},{6,2},{3,7},{7,3},{8,12},{12,8},{9,1... | collective-permute-start | bytes 1572872 | tf_op jit(solution)/shard_map/ppermute | solution.py:168
  3.6 22.3 %collective-permute-start.2 = (f32[1024,128]{1,0:T(8,128)}, f32[1024,128]{1,0:T(8,128)S(1)}, u32[]{:S(2)}, u32[]{:S(2)}) collective-permute-start(f32[1024,128]{1,0:T(8,128)} %v_ref.1), channel_id=1, source_target_pairs={{4,8},{12,16},{20,24},{28,32},{36,40},{44,48},{52,56},{60,64},{68,... | collective-permute-start | bytes 1572872 | tf_op jit(solution)/shard_map/ppermute | solution.py:164
  4.3 1.2 %copy-start.1 = (bf16[1024,512]{1,0:T(8,128)(2,1)S(1)}, bf16[1024,512]{1,0:T(8,128)(2,1)}, u32[]{:S(2)}) copy-start(bf16[1024,512]{1,0:T(8,128)(2,1)} %raw_ref.1) | copy-start | bytes 3145732
  5.5 0.7 copy-start.2
  8.5 14.5 %copy-start = (f32[1024,128]{1,0:T(8,128)S(1)}, f32[1024,128]{1,0:T(8,128)}, u32[]{:S(2)}) copy-start(f32[1024,128]{1,0:T(8,128)} %v_ref.1) | copy-start | bytes 1572868
  14.7 11.2 %collective-permute-start.3 = (f32[1024]{0:T(1024)S(1)}, f32[1024]{0:T(1024)S(1)}, u32[]{:S(2)}, u32[]{:S(2)}) collective-permute-start(f32[1024]{0:T(1024)S(1)} %add_reduce_fusion), channel_id=1, source_target_pairs={{4,8},{12,16},{20,24},{28,32},{36,40},{44,48},{52,56},{60,64},{68,... | collective-permute-start | bytes 12296 | tf_op jit(solution)/shard_map/ppermute | solution.py:164
  15.4 8.9 %collective-permute-start.5 = (f32[1024]{0:T(1024)S(1)}, f32[1024]{0:T(1024)S(1)}, u32[]{:S(2)}, u32[]{:S(2)}) collective-permute-start(f32[1024]{0:T(1024)S(1)} %get-tuple-element.81), channel_id=1, source_target_pairs={{0,4},{4,0},{1,5},{5,1},{2,6},{6,2},{3,7},{7,3},{8,12},{12,8},{9,1... | collective-permute-start | bytes 12296 | tf_op jit(solution)/shard_map/ppermute | solution.py:168
  27.7 2.2 %collective-permute-start.7 = (bf16[1024,256]{1,0:T(8,128)(2,1)S(1)}, bf16[1024,256]{1,0:T(8,128)(2,1)S(1)}, u32[]{:S(2)}, u32[]{:S(2)}) collective-permute-start(bf16[1024,256]{1,0:T(8,128)(2,1)S(1)} %pad_maximum_fusion.u_ref), channel_id=1, source_target_pairs={{0,4},{4,0},{1,5},{5,1},{2,6},{6,2},{3,7},{7,3},{8,12},{12,8},{9,1... | collective-permute-start | bytes 1572872 | tf_op jit(solution)/shard_map/ppermute | solution.py:168
  27.8 3.4 %collective-permute-start.6 = (bf16[1024,256]{1,0:T(8,128)(2,1)S(1)}, bf16[1024,256]{1,0:T(8,128)(2,1)S(1)}, u32[]{:S(2)}, u32[]{:S(2)}) collective-permute-start(bf16[1024,256]{1,0:T(8,128)(2,1)S(1)} %pad_maximum_fusion.u_ref), channel_id=1, source_target_pairs={{4,8},{12,16},{20,24},{28,32},{36,40},{44,48},{52,56},{60,64},{68,... | collective-permute-start | bytes 1572872 | tf_op jit(solution)/shard_map/ppermute | solution.py:164
  32.7 13.9 %collective-permute-start.8 = (bf16[1024,128]{1,0:T(8,128)(2,1)S(1)}, bf16[1024,128]{1,0:T(8,128)(2,1)S(1)}, u32[]{:S(2)}, u32[]{:S(2)}) collective-permute-start(bf16[1024,128]{1,0:T(8,128)(2,1)S(1)} %get-tuple-element.82), channel_id=1, source_target_pairs={{4,8},{12,16},{20,24},{28,32},{36,40},{44,48},{52,56},{60,64},{68,... | collective-permute-start | bytes 786440 | tf_op jit(solution)/shard_map/ppermute | solution.py:164
  33.5 11.9 %collective-permute-start.9 = (bf16[1024,256]{1,0:T(8,128)(2,1)S(1)}, bf16[1024,256]{1,0:T(8,128)(2,1)S(1)}, u32[]{:S(2)}, u32[]{:S(2)}) collective-permute-start(bf16[1024,256]{1,0:T(8,128)(2,1)S(1)} %pad_maximum_fusion.1.u_ref), channel_id=1, source_target_pairs={{0,4},{4,0},{1,5},{5,1},{2,6},{6,2},{3,7},{7,3},{8,12},{12,8},{9,1... | collective-permute-start | bytes 1572872 | tf_op jit(solution)/shard_map/ppermute | solution.py:168
  47.6 2.3 %collective-permute-start.10 = (f32[10,128]{1,0:T(8,128)S(1)}, f32[10,128]{1,0:T(8,128)S(1)}, u32[]{:S(2)}, u32[]{:S(2)}) collective-permute-start(f32[10,128]{1,0:T(8,128)S(1)} %stack.71), channel_id=1, source_target_pairs={{0,4},{4,0},{1,5},{5,1},{2,6},{6,2},{3,7},{7,3},{8,12},{12,8},{9,1... | collective-permute-start | bytes 15368 | tf_op jit(solution)/shard_map/ppermute | solution.py:168
